TPU v7x, 256 devices: a whole 4x4x8 slice. The times are simulated.
256 devices in a mesh: space: 64 (over x, y, z_hi), chan: 4 (over z_lo, core).
Axes of the slice: x: 4, y: 4, z: 8 (z_hi: 4, z_lo: 2; z = z_hi * 2 + z_lo), core: 2. Of those that a mesh axis runs over, the one named last changes fastest.
Arguments:
- features: bfloat16 [64, 128, 8, 8, 256], P('space'), may hold values from -6 to 6
- column_heights: int32 [64], replicated, may hold values from 1 to 32, as said below
- weight_one: bfloat16 [27, 128, 128], P(None, 'chan'), may hold values from -0.109375 to 0.109375
- bias_one: float32 [128], P('chan'), may hold values from 0 to 1
- weight_two: bfloat16 [27, 128, 128], P(None, 'chan'), may hold values from -0.109375 to 0.109375
- bias_two: float32 [128], P('chan'), may hold values from 0 to 1
Outputs:
- output: bfloat16 [64, 128, 8, 8, 256], P('space', 'chan')
Inputs may be any that keep to these rules, and one draw needn't show every extreme that they name: Column c holds its active bricks at its lowest column_heights[c] of 32 levels; some column holds exactly 32.
All inputs are finite; a program needn't handle non-finite values.
Results may differ from a plain program's by a relative error of at most 0.004.
Values may be sent and summed in bfloat16 or wider, within the bound.
A program may use at most 128 MiB of HBM per device.

v0:
```python
import jax
import jax.numpy as jnp
from jax import lax
from jax.sharding import PartitionSpec as P

COL_Y = 8


def passed_along(value, axis, by):
    peers = lax.axis_size(axis)
    pairs = [(i, i + by) for i in range(peers) if 0 <= i + by < peers]
    return lax.ppermute(value, axis, pairs)


def block_size():
    return 16


def conv_block(padded, weights, biases, offset, anchor, block_len, live_top):
    channels = padded.shape[0]
    quarter = weights.shape[1]
    summed = jnp.zeros((quarter, 64 * block_len), jnp.float32)
    for shift_x in range(3):
        for shift_y in range(3):
            for shift_z in range(3):
                sliced = lax.dynamic_slice(
                    padded, (0, shift_x, shift_y, offset + shift_z), (channels, 8, 8, block_len)
                )
                sliced = sliced.reshape(channels, 64 * block_len)
                summed = summed + jnp.dot(
                    weights[9 * shift_x + 3 * shift_y + shift_z],
                    sliced,
                    preferred_element_type=jnp.float32,
                )
    result = jax.nn.relu(summed + biases[:, None]).reshape(quarter, 8, 8, block_len)
    inside = anchor + lax.iota(jnp.int32, block_len) < live_top
    return (result * inside.astype(jnp.float32)).astype(jnp.bfloat16)


def run_blocks(
    padded, weights, biases, first_block, last_block, base_block, frame_len, block_len, live_top
):
    output = jnp.zeros((weights.shape[1], 8, 8, frame_len), jnp.bfloat16)

    def advance(block_id, output):
        start = block_id * block_len
        result = conv_block(
            padded, weights, biases, start, base_block * block_len + start, block_len, live_top
        )
        return lax.dynamic_update_slice_in_dim(output, result, start, 3)

    return lax.fori_loop(first_block, last_block, advance, output)


def border_pieces(centre, grid_row):
    found = []
    for stride in (1, -1):
        border = centre[:, :, 7] if stride == 1 else centre[:, :, 0]
        arrived = passed_along(border, "space", stride)
        retain = grid_row > 0 if stride == 1 else grid_row < COL_Y - 1
        found.append(jnp.where(retain, arrived, jnp.zeros_like(arrived)))
    widened = jnp.concatenate([found[0][:, :, None], centre, found[1][:, :, None]], axis=2)
    for stride in (COL_Y, -COL_Y):
        border = widened[:, 7] if stride > 0 else widened[:, 0]
        found.append(passed_along(border, "space", stride))
    return (found[0], found[1], found[2], found[3], widened)


def layer_input(centre_full, grid_row):
    low_y, high_y, low_x, high_x, widened = border_pieces(centre_full, grid_row)
    filled = jnp.concatenate([low_x[:, None], widened, high_x[:, None]], axis=1)
    return jnp.pad(filled, ((0, 0), (0, 0), (0, 0), (1, 1)))


def compute_layer(padded, weights, biases, column_heights, column_id, block_len, depth_cells):
    live_top = column_heights[column_id] * 8
    own_blocks = (live_top + block_len - 1) // block_len
    return run_blocks(padded, weights, biases, 0, own_blocks, 0, depth_cells, block_len, live_top)


def on_device(features, column_heights, weight_one, bias_one, weight_two, bias_two):
    column_id = lax.axis_index("space")
    depth_cells = features.shape[4]
    block_len = block_size()
    grid_row = column_id % COL_Y
    live_top = column_heights[column_id] * 8
    z_cells = lax.iota(jnp.int32, depth_cells)
    inputs = features[0] * (z_cells < live_top).astype(jnp.bfloat16)
    padded = layer_input(inputs, grid_row)
    hidden = compute_layer(
        padded, weight_one, bias_one, column_heights, column_id, block_len, depth_cells
    )
    gathered = lax.all_gather(hidden, "chan", axis=0, tiled=True)
    padded = layer_input(gathered, grid_row)
    output = compute_layer(
        padded, weight_two, bias_two, column_heights, column_id, block_len, depth_cells
    )
    return output[None]


def solution(mesh):
    placed = (
        P("space", None, None, None, None),
        P(),
        P(None, "chan", None),
        P("chan"),
        P(None, "chan", None),
        P("chan"),
    )
    return jax.shard_map(
        on_device,
        mesh=mesh,
        in_specs=placed,
        out_specs=P("space", "chan", None, None, None),
        check_vma=False,
    )
```

profile of v0, /device:TPU:3, one launch (start us, length us, event | category | flops | bytes accessed | tf_op | source)
XLA Modules:
  0.0 775.8 jit_solution(17238935889893305870)
XLA Ops:
  15.3 10.4 %collective-permute-start.1 = (bf16[128,8,256]{2,0,1:T(8,128)(2,1)S(1)}, bf16[128,8,256]{2,0,1:T(8,128)(2,1)S(1)}, u32[]{:S(2)}, u32[]{:S(2)}) collective-permute-start(bf16[128,8,256]{2,0,1:T(8,128)(2,1)S(1)} %get-tuple-element.317), channel_id=1, source_target_pairs={{4,0},{8,4},{12,8},{16,12},{20,16},{24,20},{28,24},{32,28},{36,32}... | collective-permute-start | bytes 1572872 | tf_op jit(solution)/shard_map/ppermute | solution.py:12
  27.6 20.0 %collective-permute-done.1 = bf16[128,8,256]{2,0,1:T(8,128)(2,1)S(1)} collective-permute-done((bf16[128,8,256]{2,0,1:T(8,128)(2,1)S(1)}, bf16[128,8,256]{2,0,1:T(8,128)(2,1)S(1)}, u32[]{:S(2)}, u32[]{:S(2)}) %collective-permute-start.1) | collective-permute-done | bytes 524320 | tf_op jit(solution)/shard_map/ppermute | solution.py:12
  65.5 21.0 %collective-permute-done.2 = bf16[128,10,256]{2,0,1:T(8,128)(2,1)S(1)} collective-permute-done((bf16[128,10,256]{2,0,1:T(8,128)(2,1)}, bf16[128,10,256]{2,0,1:T(8,128)(2,1)S(1)}, u32[]{:S(2)}, u32[]{:S(2)}) %collective-permute-start.2) | collective-permute-done | bytes 655392 | tf_op jit(solution)/shard_map/ppermute | solution.py:12
  99.2 9.5 %copy.41 = bf16[128,10,10,256]{0,3,2,1:T(8,128)(2,1)} copy(bf16[128,10,10,256]{3,0,2,1:T(8,128)(2,1)} %pad_maximum_fusion) | data formatting | bytes 13107200
  120.1 250.0 %while.24 = (s32[]{:T(128)}, bf16[32,8,8,256]{0,3,2,1:T(8,128)(2,1)}, s32[]{:T(128)}, bf16[128,10,10,258]{0,3,2,1:T(8,128)(2,1)}, bf16[27,32,128]{2,1,0:T(8,128)...) while((s32[]{:T(128)}, ...), condition=%wide.region_1.2_spmd, body=%wide.region_0.1_spmd.sunk | while | flops 227475520 | bytes 29057992 | solution.py:52
  135.3 9.0 %constant_dynamic-slice_fusion.56 = (bf16[128,8,8,16]{0,3,2,1:T(8,128)(2,1)S(1)}, bf16[128,8,8,16]{0,3,2,1:T(8,128)(2,1)S(1)}, bf16[128,8,8,16]{0,3,2,1:T(8,128)...) fusion(bf16[128,10,10,258]{0,3,2,1:T(8,128)(2,1)} %get-tuple-el, ...), kind=kLoop, calls=%fused_computation.105.clone.1 | loop fusion | bytes 14155788 | tf_op jit(solution)/shard_map/while/body/dynamic_slice | solution.py:26
  150.8 9.5 %constant_dynamic-slice_fusion.56 = (bf16[128,8,8,16]{0,3,2,1:T(8,128)(2,1)S(1)}, bf16[128,8,8,16]{0,3,2,1:T(8,128)(2,1)S(1)}, bf16[128,8,8,16]{0,3,2,1:T(8,128)...) fusion(bf16[128,10,10,258]{0,3,2,1:T(8,128)(2,1)} %get-tuple-el, ...), kind=kLoop, calls=%fused_computation.105.clone.1 | loop fusion | bytes 14155788 | tf_op jit(solution)/shard_map/while/body/dynamic_slice | solution.py:26
  181.5 9.4 %constant_dynamic-slice_fusion.56 = (bf16[128,8,8,16]{0,3,2,1:T(8,128)(2,1)S(1)}, bf16[128,8,8,16]{0,3,2,1:T(8,128)(2,1)S(1)}, bf16[128,8,8,16]{0,3,2,1:T(8,128)...) fusion(bf16[128,10,10,258]{0,3,2,1:T(8,128)(2,1)} %get-tuple-el, ...), kind=kLoop, calls=%fused_computation.105.clone.1 | loop fusion | bytes 14155788 | tf_op jit(solution)/shard_map/while/body/dynamic_slice | solution.py:26
  197.4 8.9 %constant_dynamic-slice_fusion.56 = (bf16[128,8,8,16]{0,3,2,1:T(8,128)(2,1)S(1)}, bf16[128,8,8,16]{0,3,2,1:T(8,128)(2,1)S(1)}, bf16[128,8,8,16]{0,3,2,1:T(8,128)...) fusion(bf16[128,10,10,258]{0,3,2,1:T(8,128)(2,1)} %get-tuple-el, ...), kind=kLoop, calls=%fused_computation.105.clone.1 | loop fusion | bytes 14155788 | tf_op jit(solution)/shard_map/while/body/dynamic_slice | solution.py:26
  212.8 9.0 %constant_dynamic-slice_fusion.56 = (bf16[128,8,8,16]{0,3,2,1:T(8,128)(2,1)S(1)}, bf16[128,8,8,16]{0,3,2,1:T(8,128)(2,1)S(1)}, bf16[128,8,8,16]{0,3,2,1:T(8,128)...) fusion(bf16[128,10,10,258]{0,3,2,1:T(8,128)(2,1)} %get-tuple-el, ...), kind=kLoop, calls=%fused_computation.105.clone.1 | loop fusion | bytes 14155788 | tf_op jit(solution)/shard_map/while/body/dynamic_slice | solution.py:26
  243.4 8.8 %constant_dynamic-slice_fusion.56 = (bf16[128,8,8,16]{0,3,2,1:T(8,128)(2,1)S(1)}, bf16[128,8,8,16]{0,3,2,1:T(8,128)(2,1)S(1)}, bf16[128,8,8,16]{0,3,2,1:T(8,128)...) fusion(bf16[128,10,10,258]{0,3,2,1:T(8,128)(2,1)} %get-tuple-el, ...), kind=kLoop, calls=%fused_computation.105.clone.1 | loop fusion | bytes 14155788 | tf_op jit(solution)/shard_map/while/body/dynamic_slice | solution.py:26
  273.7 9.6 %constant_dynamic-slice_fusion.56 = (bf16[128,8,8,16]{0,3,2,1:T(8,128)(2,1)S(1)}, bf16[128,8,8,16]{0,3,2,1:T(8,128)(2,1)S(1)}, bf16[128,8,8,16]{0,3,2,1:T(8,128)...) fusion(bf16[128,10,10,258]{0,3,2,1:T(8,128)(2,1)} %get-tuple-el, ...), kind=kLoop, calls=%fused_computation.105.clone.1 | loop fusion | bytes 14155788 | tf_op jit(solution)/shard_map/while/body/dynamic_slice | solution.py:26
  289.9 9.1 %constant_dynamic-slice_fusion.56 = (bf16[128,8,8,16]{0,3,2,1:T(8,128)(2,1)S(1)}, bf16[128,8,8,16]{0,3,2,1:T(8,128)(2,1)S(1)}, bf16[128,8,8,16]{0,3,2,1:T(8,128)...) fusion(bf16[128,10,10,258]{0,3,2,1:T(8,128)(2,1)} %get-tuple-el, ...), kind=kLoop, calls=%fused_computation.105.clone.1 | loop fusion | bytes 14155788 | tf_op jit(solution)/shard_map/while/body/dynamic_slice | solution.py:26
  305.5 10.9 %constant_dynamic-slice_fusion.56 = (bf16[128,8,8,16]{0,3,2,1:T(8,128)(2,1)S(1)}, bf16[128,8,8,16]{0,3,2,1:T(8,128)(2,1)S(1)}, bf16[128,8,8,16]{0,3,2,1:T(8,128)...) fusion(bf16[128,10,10,258]{0,3,2,1:T(8,128)(2,1)} %get-tuple-el, ...), kind=kLoop, calls=%fused_computation.105.clone.1 | loop fusion | bytes 14155788 | tf_op jit(solution)/shard_map/while/body/dynamic_slice | solution.py:26
  338.0 9.4 %constant_dynamic-slice_fusion.56 = (bf16[128,8,8,16]{0,3,2,1:T(8,128)(2,1)S(1)}, bf16[128,8,8,16]{0,3,2,1:T(8,128)(2,1)S(1)}, bf16[128,8,8,16]{0,3,2,1:T(8,128)...) fusion(bf16[128,10,10,258]{0,3,2,1:T(8,128)(2,1)} %get-tuple-el, ...), kind=kLoop, calls=%fused_computation.105.clone.1 | loop fusion | bytes 14155788 | tf_op jit(solution)/shard_map/while/body/dynamic_slice | solution.py:26
  354.0 9.6 %constant_dynamic-slice_fusion.56 = (bf16[128,8,8,16]{0,3,2,1:T(8,128)(2,1)S(1)}, bf16[128,8,8,16]{0,3,2,1:T(8,128)(2,1)S(1)}, bf16[128,8,8,16]{0,3,2,1:T(8,128)...) fusion(bf16[128,10,10,258]{0,3,2,1:T(8,128)(2,1)} %get-tuple-el, ...), kind=kLoop, calls=%fused_computation.105.clone.1 | loop fusion | bytes 14155788 | tf_op jit(solution)/shard_map/while/body/dynamic_slice | solution.py:26
  374.7 41.7 %all-gather.2.cloned.1.call-done = bf16[128,8,8,256]{3,0,1,2:T(8,128)(2,1)} async-done(((bf16[32,8,8,256]{3,0,1,2:T(8,128)(2,1)}), bf16[128,8,8,256]{3,0,1,2:T(8,128)(2,1)}) %all-gather.2.cloned.1.call-update) | async-done | bytes 4194320 | tf_op jit(solution)/shard_map/all_gather | solution.py:93
  428.4 13.0 %collective-permute-done.4 = bf16[128,8,256]{2,0,1:T(8,128)(2,1)S(1)} collective-permute-done((bf16[128,8,256]{2,0,1:T(8,128)(2,1)S(1)}, bf16[128,8,256]{2,0,1:T(8,128)(2,1)S(1)}, u32[]{:S(2)}, u32[]{:S(2)}) %collective-permute-start.4) | collective-permute-done | bytes 524320 | tf_op jit(solution)/shard_map/ppermute | solution.py:12
  441.4 9.7 %collective-permute-done.5 = bf16[128,8,256]{2,0,1:T(8,128)(2,1)S(1)} collective-permute-done((bf16[128,8,256]{2,0,1:T(8,128)(2,1)S(1)}, bf16[128,8,256]{2,0,1:T(8,128)(2,1)S(1)}, u32[]{:S(2)}, u32[]{:S(2)}) %collective-permute-start.5) | collective-permute-done | bytes 524320 | tf_op jit(solution)/shard_map/ppermute | solution.py:12
  459.8 23.8 %collective-permute-done.6 = bf16[128,10,256]{2,0,1:T(8,128)(2,1)S(1)} collective-permute-done((bf16[128,10,256]{2,0,1:T(8,128)(2,1)}, bf16[128,10,256]{2,0,1:T(8,128)(2,1)S(1)}, u32[]{:S(2)}, u32[]{:S(2)}) %collective-permute-start.6) | collective-permute-done | bytes 655392 | tf_op jit(solution)/shard_map/ppermute | solution.py:12
  493.2 9.6 %copy.42 = bf16[128,10,10,256]{0,3,2,1:T(8,128)(2,1)} copy(bf16[128,10,10,256]{3,0,1,2:T(8,128)(2,1)} %pad_maximum_fusion.1) | data formatting | bytes 13107200
  514.1 250.0 %while.25 = (s32[]{:T(128)}, bf16[32,8,8,256]{0,3,2,1:T(8,128)(2,1)}, s32[]{:T(128)}, bf16[128,10,10,258]{0,3,2,1:T(8,128)(2,1)}, bf16[27,32,128]{2,1,0:T(8,128)...) while((s32[]{:T(128)}, ...), condition=%wide.region_3.4_spmd, body=%wide.region_2.3_spmd.sunk | while | flops 227475520 | bytes 29057992 | solution.py:52
  529.3 9.0 %constant_dynamic-slice_fusion.57 = (bf16[128,8,8,16]{0,3,2,1:T(8,128)(2,1)S(1)}, bf16[128,8,8,16]{0,3,2,1:T(8,128)(2,1)S(1)}, bf16[128,8,8,16]{0,3,2,1:T(8,128)...) fusion(bf16[128,10,10,258]{0,3,2,1:T(8,128)(2,1)} %get-tuple-el, ...), kind=kLoop, calls=%fused_computation.229.clone.1 | loop fusion | bytes 14155788 | tf_op jit(solution)/shard_map/while/body/dynamic_slice | solution.py:26
  544.8 9.5 %constant_dynamic-slice_fusion.57 = (bf16[128,8,8,16]{0,3,2,1:T(8,128)(2,1)S(1)}, bf16[128,8,8,16]{0,3,2,1:T(8,128)(2,1)S(1)}, bf16[128,8,8,16]{0,3,2,1:T(8,128)...) fusion(bf16[128,10,10,258]{0,3,2,1:T(8,128)(2,1)} %get-tuple-el, ...), kind=kLoop, calls=%fused_computation.229.clone.1 | loop fusion | bytes 14155788 | tf_op jit(solution)/shard_map/while/body/dynamic_slice | solution.py:26
  575.5 9.4 %constant_dynamic-slice_fusion.57 = (bf16[128,8,8,16]{0,3,2,1:T(8,128)(2,1)S(1)}, bf16[128,8,8,16]{0,3,2,1:T(8,128)(2,1)S(1)}, bf16[128,8,8,16]{0,3,2,1:T(8,128)...) fusion(bf16[128,10,10,258]{0,3,2,1:T(8,128)(2,1)} %get-tuple-el, ...), kind=kLoop, calls=%fused_computation.229.clone.1 | loop fusion | bytes 14155788 | tf_op jit(solution)/shard_map/while/body/dynamic_slice | solution.py:26
  591.4 8.9 %constant_dynamic-slice_fusion.57 = (bf16[128,8,8,16]{0,3,2,1:T(8,128)(2,1)S(1)}, bf16[128,8,8,16]{0,3,2,1:T(8,128)(2,1)S(1)}, bf16[128,8,8,16]{0,3,2,1:T(8,128)...) fusion(bf16[128,10,10,258]{0,3,2,1:T(8,128)(2,1)} %get-tuple-el, ...), kind=kLoop, calls=%fused_computation.229.clone.1 | loop fusion | bytes 14155788 | tf_op jit(solution)/shard_map/while/body/dynamic_slice | solution.py:26
  606.8 9.0 %constant_dynamic-slice_fusion.57 = (bf16[128,8,8,16]{0,3,2,1:T(8,128)(2,1)S(1)}, bf16[128,8,8,16]{0,3,2,1:T(8,128)(2,1)S(1)}, bf16[128,8,8,16]{0,3,2,1:T(8,128)...) fusion(bf16[128,10,10,258]{0,3,2,1:T(8,128)(2,1)} %get-tuple-el, ...), kind=kLoop, calls=%fused_computation.229.clone.1 | loop fusion | bytes 14155788 | tf_op jit(solution)/shard_map/while/body/dynamic_slice | solution.py:26
  667.7 9.6 %constant_dynamic-slice_fusion.57 = (bf16[128,8,8,16]{0,3,2,1:T(8,128)(2,1)S(1)}, bf16[128,8,8,16]{0,3,2,1:T(8,128)(2,1)S(1)}, bf16[128,8,8,16]{0,3,2,1:T(8,128)...) fusion(bf16[128,10,10,258]{0,3,2,1:T(8,128)(2,1)} %get-tuple-el, ...), kind=kLoop, calls=%fused_computation.229.clone.1 | loop fusion | bytes 14155788 | tf_op jit(solution)/shard_map/while/body/dynamic_slice | solution.py:26
  683.9 9.1 %constant_dynamic-slice_fusion.57 = (bf16[128,8,8,16]{0,3,2,1:T(8,128)(2,1)S(1)}, bf16[128,8,8,16]{0,3,2,1:T(8,128)(2,1)S(1)}, bf16[128,8,8,16]{0,3,2,1:T(8,128)...) fusion(bf16[128,10,10,258]{0,3,2,1:T(8,128)(2,1)} %get-tuple-el, ...), kind=kLoop, calls=%fused_computation.229.clone.1 | loop fusion | bytes 14155788 | tf_op jit(solution)/shard_map/while/body/dynamic_slice | solution.py:26
  699.5 10.9 %constant_dynamic-slice_fusion.57 = (bf16[128,8,8,16]{0,3,2,1:T(8,128)(2,1)S(1)}, bf16[128,8,8,16]{0,3,2,1:T(8,128)(2,1)S(1)}, bf16[128,8,8,16]{0,3,2,1:T(8,128)...) fusion(bf16[128,10,10,258]{0,3,2,1:T(8,128)(2,1)} %get-tuple-el, ...), kind=kLoop, calls=%fused_computation.229.clone.1 | loop fusion | bytes 14155788 | tf_op jit(solution)/shard_map/while/body/dynamic_slice | solution.py:26
  732.0 9.4 %constant_dynamic-slice_fusion.57 = (bf16[128,8,8,16]{0,3,2,1:T(8,128)(2,1)S(1)}, bf16[128,8,8,16]{0,3,2,1:T(8,128)(2,1)S(1)}, bf16[128,8,8,16]{0,3,2,1:T(8,128)...) fusion(bf16[128,10,10,258]{0,3,2,1:T(8,128)(2,1)} %get-tuple-el, ...), kind=kLoop, calls=%fused_computation.229.clone.1 | loop fusion | bytes 14155788 | tf_op jit(solution)/shard_map/while/body/dynamic_slice | solution.py:26
  748.0 9.6 %constant_dynamic-slice_fusion.57 = (bf16[128,8,8,16]{0,3,2,1:T(8,128)(2,1)S(1)}, bf16[128,8,8,16]{0,3,2,1:T(8,128)(2,1)S(1)}, bf16[128,8,8,16]{0,3,2,1:T(8,128)...) fusion(bf16[128,10,10,258]{0,3,2,1:T(8,128)(2,1)} %get-tuple-el, ...), kind=kLoop, calls=%fused_computation.229.clone.1 | loop fusion | bytes 14155788 | tf_op jit(solution)/shard_map/while/body/dynamic_slice | solution.py:26
  (1012 shorter events, 403.7 us)
Async XLA Ops:
  6.5 409.9 %all-gather.2.cloned.1.call-start = ((), (), s32[]{:S(2)}) async-start(), calls=%async_computation | async-start | bytes 5242880 | tf_op jit(solution)/shard_map/all_gather | solution.py:93
  15.3 32.3 %collective-permute-start.1 = (bf16[128,8,256]{2,0,1:T(8,128)(2,1)S(1)}, bf16[128,8,256]{2,0,1:T(8,128)(2,1)S(1)}, u32[]{:S(2)}, u32[]{:S(2)}) collective-permute-start(bf16[128,8,256]{2,0,1:T(8,128)(2,1)S(1)} %get-tuple-element.317), channel_id=1, source_target_pairs={{4,0},{8,4},{12,8},{16,12},{20,16},{24,20},{28,24},{32,28},{36,32}... | collective-permute-start | bytes 1572872 | tf_op jit(solution)/shard_map/ppermute | solution.py:12
  25.7 29.7 %collective-permute-start = (bf16[128,8,256]{2,0,1:T(8,128)(2,1)S(1)}, bf16[128,8,256]{2,0,1:T(8,128)(2,1)S(1)}, u32[]{:S(2)}, u32[]{:S(2)}) collective-permute-start(bf16[128,8,256]{2,0,1:T(8,128)(2,1)S(1)} %get-tuple-element.316), channel_id=1, source_target_pairs={{0,4},{4,8},{8,12},{12,16},{16,20},{20,24},{24,28},{28,32},{32,36}... | collective-permute-start | bytes 1572872 | tf_op jit(solution)/shard_map/ppermute | solution.py:12
  57.8 28.7 %collective-permute-start.2 = (bf16[128,10,256]{2,0,1:T(8,128)(2,1)}, bf16[128,10,256]{2,0,1:T(8,128)(2,1)S(1)}, u32[]{:S(2)}, u32[]{:S(2)}) collective-permute-start(bf16[128,10,256]{2,0,1:T(8,128)(2,1)} %get-tuple-element.312), channel_id=1, source_target_pairs={{0,32},{4,36},{8,40},{12,44},{16,48},{20,52},{24,56},{28,60},{32,6... | collective-permute-start | bytes 1966088 | tf_op jit(solution)/shard_map/ppermute | solution.py:12
  59.7 33.3 %collective-permute-start.3 = (bf16[128,10,256]{2,0,1:T(8,128)(2,1)S(1)}, bf16[128,10,256]{2,0,1:T(8,128)(2,1)S(1)}, u32[]{:S(2)}, u32[]{:S(2)}) collective-permute-start(bf16[128,10,256]{2,0,1:T(8,128)(2,1)S(1)} %get-tuple-element.313), channel_id=1, source_target_pairs={{32,0},{36,4},{40,8},{44,12},{48,16},{52,20},{56,24},{60,28},{64,3... | collective-permute-start | bytes 1966088 | tf_op jit(solution)/shard_map/ppermute | solution.py:12
  117.0 3.1 copy-start.1
  117.0 3.1 copy-start.3
  416.4 34.7 %copy-start = (bf16[128,8,8,256]{3,0,1,2:T(8,128)(2,1)S(1)}, bf16[128,8,8,256]{3,0,1,2:T(8,128)(2,1)}, u32[]{:S(2)}) copy-start(bf16[128,8,8,256]{3,0,1,2:T(8,128)(2,1)} %all-gather.2.cloned.1.call-done) | copy-start | bytes 12582916
  417.9 23.5 %collective-permute-start.4 = (bf16[128,8,256]{2,0,1:T(8,128)(2,1)S(1)}, bf16[128,8,256]{2,0,1:T(8,128)(2,1)S(1)}, u32[]{:S(2)}, u32[]{:S(2)}) collective-permute-start(bf16[128,8,256]{2,0,1:T(8,128)(2,1)S(1)} %get-tuple-element.314), channel_id=1, source_target_pairs={{0,4},{4,8},{8,12},{12,16},{16,20},{20,24},{24,28},{28,32},{32,36}... | collective-permute-start | bytes 1572872 | tf_op jit(solution)/shard_map/ppermute | solution.py:12
  422.2 28.9 %collective-permute-start.5 = (bf16[128,8,256]{2,0,1:T(8,128)(2,1)S(1)}, bf16[128,8,256]{2,0,1:T(8,128)(2,1)S(1)}, u32[]{:S(2)}, u32[]{:S(2)}) collective-permute-start(bf16[128,8,256]{2,0,1:T(8,128)(2,1)S(1)} %get-tuple-element.315), channel_id=1, source_target_pairs={{4,0},{8,4},{12,8},{16,12},{20,16},{24,20},{28,24},{32,28},{36,32}... | collective-permute-start | bytes 1572872 | tf_op jit(solution)/shard_map/ppermute | solution.py:12
  452.1 31.5 %collective-permute-start.6 = (bf16[128,10,256]{2,0,1:T(8,128)(2,1)}, bf16[128,10,256]{2,0,1:T(8,128)(2,1)S(1)}, u32[]{:S(2)}, u32[]{:S(2)}) collective-permute-start(bf16[128,10,256]{2,0,1:T(8,128)(2,1)} %get-tuple-element.310), channel_id=1, source_target_pairs={{0,32},{4,36},{8,40},{12,44},{16,48},{20,52},{24,56},{28,60},{32,6... | collective-permute-start | bytes 1966088 | tf_op jit(solution)/shard_map/ppermute | solution.py:12
  455.9 31.5 %collective-permute-start.7 = (bf16[128,10,256]{2,0,1:T(8,128)(2,1)S(1)}, bf16[128,10,256]{2,0,1:T(8,128)(2,1)S(1)}, u32[]{:S(2)}, u32[]{:S(2)}) collective-permute-start(bf16[128,10,256]{2,0,1:T(8,128)(2,1)S(1)} %get-tuple-element.311), channel_id=1, source_target_pairs={{32,0},{36,4},{40,8},{44,12},{48,16},{52,20},{56,24},{60,28},{64,3... | collective-permute-start | bytes 1966088 | tf_op jit(solution)/shard_map/ppermute | solution.py:12
  511.0 3.1 copy-start.2
  511.0 3.1 copy-start.4
Sparse Core Ops, SparseCore 0:
  374.8 41.5 all-gather.1
where the time goes:
time: 777 us; the launch traced here: 776 us
  local copies, waits for them, and re-layouts  351 us (45%)
  matrix products  174 us (22%)
  waiting for transfers between devices  147 us (19%)
  other arithmetic  50 us (6%)
  starting transfers between devices  38.2 us (5%)
  between operations  14.2 us (2%)
    dynamic_slice x32, local copies, waits for them, and re-layouts, conv_block(): lax.dynamic_slice(padded, (0, shift_x, shift_y, offset + shift_z), (chann...  291 us
    dot_general x864, matrix products, conv_block(): jnp.dot(weights[9 * shift_x + 3 * shift_y + shift_z], sliced, preferred_e...  174 us
    ppermute x8, waiting for transfers between devices, passed_along(): return lax.ppermute(value, axis, pairs)  105 us
    all_gather x1, waiting for transfers between devices, on_device(): gathered = lax.all_gather(hidden, 'chan', axis=0, tiled=True)  41.7 us
    ppermute x8, starting transfers between devices, passed_along(): return lax.ppermute(value, axis, pairs)  38.2 us
    dynamic_update_slice x32, other arithmetic, advance(): return lax.dynamic_update_slice_in_dim(output, result, start, 3)  27.3 us
    unnamed x12, local copies, waits for them, and re-layouts  19.1 us
    pad x2, local copies, waits for them, and re-layouts, layer_input(): return jnp.pad(filled, ((0, 0), (0, 0), (0, 0), (1, 1)))  16.5 us
  transfers between devices with their start and end apart: 9, of which 9 were waited for; matrix products, arithmetic and copies ran while one was open for 0% of the time, Pallas kernels for 0%

commit v1 on v0

v1 whole, which is shorter than its diff:
```python
import functools

import jax
import jax.numpy as jnp
from jax import lax
from jax.experimental import pallas as pl
from jax.experimental.pallas import tpu as pltpu
from jax.sharding import PartitionSpec as P

COL_Y = 8
MESH = pl.DeviceIdType.MESH
DIRECTIONS = [(dx, dy) for dx in (-1, 0, 1) for dy in (-1, 0, 1) if (dx, dy) != (0, 0)]


def kernel(
    grid_x,
    grid_y,
    feat,
    heights,
    w_one,
    w_two,
    b_one,
    b_two,
    out,
    xx,
    stage,
    wall,
    bme,
    ball,
    bias,
    obuf,
    feat_sem,
    wl_sem,
    w_send,
    w_recv,
    b_send,
    b_recv,
    f_send,
    f_recv,
    h_send,
    h_recv,
    o_send,
    o_recv,
    o_local,
):
    column = lax.axis_index("space")
    chan = lax.axis_index("chan")
    core = chan % 2
    half = chan // 2
    col_x = column // grid_y
    col_y = column % grid_y
    fine_x = 2 * col_x + core
    fine_y = 2 * col_y + half
    depth = xx.shape[-1]
    base_y = 4 * half

    def inside(dx, dy):
        fx, fy = fine_x + dx, fine_y + dy
        return (fx >= 0) & (fx < 2 * grid_x) & (fy >= 0) & (fy < 2 * grid_y)

    def device_at(dx, dy):
        fx, fy = fine_x + dx, fine_y + dy
        return ((fx // 2) * grid_y + fy // 2, (fy % 2) * 2 + fx % 2)

    out_x = 2 * core - 1
    out_y = 2 * half - 1
    siblings = [
        (column, half * 2 + 1 - core),
        (column, (1 - half) * 2 + core),
        (column, (1 - half) * 2 + 1 - core),
    ]

    def feature_load(xl):
        return pltpu.make_async_copy(
            feat.at[0, :, 3 * core + xl], stage.at[xl], feat_sem.at[xl]
        )

    for xl in range(5):
        feature_load(xl).start()
    weights = (w_one, w_two)
    for layer in range(2):
        pltpu.make_async_copy(
            weights[layer], wall.at[layer, chan], wl_sem.at[layer]
        ).start()

    barrier = pltpu.get_barrier_semaphore()
    for dx, dy in DIRECTIONS:

        @pl.when(inside(dx, dy))
        def _():
            pl.semaphore_signal(
                barrier, inc=1, device_id=device_at(dx, dy), device_id_type=MESH
            )

    bme[...] = jnp.zeros_like(bme)
    bme[0:1, 0:32] = b_one[...]
    bme[1:2, 0:32] = b_two[...]

    peers = sum(inside(dx, dy).astype(jnp.int32) for dx, dy in DIRECTIONS)
    pl.semaphore_wait(barrier, peers)

    def weight_send(layer, k):
        return pltpu.make_async_remote_copy(
            src_ref=weights[layer],
            dst_ref=wall.at[layer, chan],
            send_sem=w_send.at[layer, k],
            recv_sem=w_recv.at[layer, k],
            device_id=siblings[k],
            device_id_type=MESH,
        )

    def bias_send(k):
        return pltpu.make_async_remote_copy(
            src_ref=bme,
            dst_ref=ball.at[chan],
            send_sem=b_send.at[k],
            recv_sem=b_recv.at[k],
            device_id=siblings[k],
            device_id_type=MESH,
        )

    for k in range(3):
        weight_send(0, k).start()
        bias_send(k).start()
    ball[chan] = bme[...]

    has_x = (col_x + out_x >= 0) & (col_x + out_x < grid_x)
    has_y = (col_y + out_y >= 0) & (col_y + out_y < grid_y)
    live_top = heights[column] * 8
    lanes = lax.broadcasted_iota(jnp.int32, (1, 1, depth), 2)
    live_row = jnp.where(lanes < live_top, 1.0, 0.0).astype(jnp.bfloat16)

    def feature_send(k):
        src_x, dst_x = 1 + 3 * core, 5 - 5 * core
        src_y, dst_y = 1 + 7 * half, 9 - 9 * half
        if k == 0:
            run = pl.ds(1 + 3 * half, 5)
            src, dst = xx.at[0, src_x, run], xx.at[0, dst_x, run]
            target = device_at(out_x, 0)
        elif k == 1:
            run = pl.ds(1 - core, 5)
            src, dst = xx.at[0, run, src_y], xx.at[0, run, dst_y]
            target = device_at(0, out_y)
        else:
            src, dst = xx.at[0, src_x, src_y], xx.at[0, dst_x, dst_y]
            target = device_at(out_x, out_y)
        return pltpu.make_async_remote_copy(
            src_ref=src,
            dst_ref=dst,
            send_sem=f_send.at[k],
            recv_sem=f_recv.at[k],
            device_id=target,
            device_id_type=MESH,
        )

    feature_when = (has_x, has_y, has_x & has_y)

    def turn(i, carry):
        xl = 4 * core + (1 - 2 * core) * i
        feature_load(xl).wait()
        value = stage[xl] * live_row
        xx[0, xl + 1 - core, 1:9] = jnp.transpose(value, (1, 0, 2))

        @pl.when(i == 0)
        def _():
            for k in (0, 2):

                @pl.when(feature_when[k])
                def _():
                    feature_send(k).start()

        return carry

    lax.fori_loop(0, 5, turn, 0)

    @pl.when(has_y)
    def _():
        feature_send(1).start()

    for k in range(3):
        weight_send(1, k).start()

    @pl.when(jnp.logical_not(has_x))
    def _():
        for layer in range(2):

            def clear(y, carry):
                xx[layer, 5 * core, y] = jnp.zeros((xx.shape[3], depth), xx.dtype)
                return carry

            lax.fori_loop(0, 10, clear, 0)

    @pl.when(jnp.logical_not(has_y))
    def _():
        for layer in range(2):

            def clear(x, carry):
                xx[layer, x, 9 * half] = jnp.zeros((xx.shape[3], depth), xx.dtype)
                return carry

            lax.fori_loop(0, 6, clear, 0)

    pltpu.make_async_copy(w_one, wall.at[0, chan], wl_sem.at[0]).wait()
    for k in range(3):
        bias_send(k).wait_recv()
        weight_send(0, k).wait_recv()
    rows = lax.broadcasted_iota(jnp.int32, (32, 128), 0)
    cols = lax.broadcasted_iota(jnp.int32, (32, 128), 1)
    for layer in range(2):
        for c in range(4):
            spread = jnp.broadcast_to(ball[c, layer : layer + 1, :], (32, 128))
            column_of = jnp.sum(
                jnp.where(rows == cols, spread, 0.0), axis=1, keepdims=True
            )
            bias[layer, 32 * c : 32 * c + 32] = jnp.broadcast_to(column_of, (32, 128))

    lane = lax.broadcasted_iota(jnp.int32, (128, depth), 1)

    def convolve(layer, px, py):
        rhs = jnp.concatenate(
            [xx[layer, px + i, base_y + py + j] for i in range(3) for j in range(3)],
            axis=0,
        )
        lhs = jnp.concatenate(
            [
                jnp.concatenate([wall[layer, c, 3 * t + k] for t in range(9)], axis=1)
                for k in range(3)
                for c in range(4)
            ],
            axis=0,
        )
        part = jnp.dot(lhs, rhs, preferred_element_type=jnp.float32)
        low = jnp.where(lane == 0, 0.0, pltpu.roll(part[0:128], 1, 1))
        high = jnp.where(lane == depth - 1, 0.0, pltpu.roll(part[256:384], depth - 1, 1))
        column_of = bias[layer]
        total = part[128:256] + low + high + jnp.concatenate([column_of] * (depth // 128), axis=1)
        total = jnp.where(lane < live_top, jnp.maximum(total, 0.0), 0.0)
        return total.astype(jnp.bfloat16)

    def first_place(n):
        late, last = n // 9, n // 13
        u = (1 - late) * (n // 3) + late * ((1 - last) * 3 + last * (n - 13))
        v = (1 - late) * (n % 3) + late * ((1 - last) * (n - 9) + last * 3)
        return (
            (1 - core) * 3 + (2 * core - 1) * u,
            (1 - half) * 3 + (2 * half - 1) * v,
        )

    def second_place(n):
        b, m = n // 4, n % 4
        e0, e3 = (3 - b) // 3, b // 3
        e2 = b // 2 - e3
        e1 = 1 - e0 - e2 - e3
        px = (e0 + e3) * (1 + m // 2) + 3 * e2
        py = e0 * (1 + m % 2) + (e1 + e2) * m + e3 * 3 * (m % 2)
        return px, py

    def hidden_send(d):
        dx, dy = DIRECTIONS[d]
        there = (fine_y + dy) % 2
        if dx == 0:
            src_x = dst_x = pl.ds(1, 4)
        else:
            src_x, dst_x = (4, 0) if dx > 0 else (1, 5)
        if dy == 0:
            src_y = dst_y = pl.ds(base_y + 1, 4)
        else:
            src_y = base_y + (4 if dy > 0 else 1)
            dst_y = 4 * there + (0 if dy > 0 else 5)
        return pltpu.make_async_remote_copy(
            src_ref=xx.at[1, src_x, src_y],
            dst_ref=xx.at[1, dst_x, dst_y],
            send_sem=h_send.at[d],
            recv_sem=h_recv.at[d],
            device_id=device_at(dx, dy),
            device_id_type=MESH,
        )

    def output_send(k, row=None):
        target = siblings[k]
        if row is None:
            src = obuf.at[target[1]]
            dst = out.at[pl.ds(4 * core, 4), pl.ds(4 * half, 4)]
        else:
            src = obuf.at[target[1], row]
            dst = out.at[4 * core + row, pl.ds(4 * half, 4)]
        return pltpu.make_async_remote_copy(
            src_ref=src,
            dst_ref=dst,
            send_sem=o_send.at[k],
            recv_sem=o_recv.at[k],
            device_id=target,
            device_id_type=MESH,
        )

    def first_pair(t, carry):
        @pl.when(t == 4)
        def _():
            for k in range(3):

                @pl.when(feature_when[k])
                def _():
                    feature_send(k).wait_recv()

        for q in range(2):
            px, py = first_place(2 * t + q)
            xx[1, px + 1, base_y + py + 1] = convolve(0, px, py)
        return carry

    lax.fori_loop(0, 8, first_pair, 0)

    for d, (dx, dy) in enumerate(DIRECTIONS):

        @pl.when(inside(dx, dy))
        def _():
            hidden_send(d).start()

    pltpu.make_async_copy(w_two, wall.at[1, chan], wl_sem.at[1]).wait()
    for k in range(3):
        weight_send(1, k).wait_recv()

    def second_pair(t, carry):
        @pl.when(t == 2)
        def _():
            for d, (dx, dy) in enumerate(DIRECTIONS):

                @pl.when(inside(-dx, -dy))
                def _():
                    hidden_send(d).wait_recv()

        for q in range(2):
            px, py = second_place(2 * t + q)
            value = convolve(1, px, py)
            for c in range(4):
                obuf[c, px, py] = value[32 * c : 32 * c + 32]

        for step, row in ((3, 0), (5, 3), (6, 1), (7, 2)):

            @pl.when(t == step)
            def _():
                for k in range(3):
                    output_send(k, row).start()

        return carry

    lax.fori_loop(0, 8, second_pair, 0)

    own = pltpu.make_async_copy(
        obuf.at[chan], out.at[pl.ds(4 * core, 4), pl.ds(4 * half, 4)], o_local
    )
    own.start()
    own.wait()
    for k in range(3):
        output_send(k).wait_recv()
    for k in range(3):
        output_send(k).wait_send()
        bias_send(k).wait_send()
        for layer in range(2):
            weight_send(layer, k).wait_send()

        @pl.when(feature_when[k])
        def _():
            feature_send(k).wait_send()

    for d, (dx, dy) in enumerate(DIRECTIONS):

        @pl.when(inside(dx, dy))
        def _():
            hidden_send(d).wait_send()


def on_device(features, column_heights, weight_one, bias_one, weight_two, bias_two):
    columns = lax.axis_size("space")
    depth = features.shape[4]
    bf16, f32 = jnp.bfloat16, jnp.float32
    anywhere = pl.BlockSpec(memory_space=pl.ANY)
    vmem = pl.BlockSpec(memory_space=pltpu.VMEM)
    smem = pl.BlockSpec(memory_space=pltpu.SMEM)
    dma = pltpu.SemaphoreType.DMA
    gathered = pl.pallas_call(
        functools.partial(kernel, columns // COL_Y, COL_Y),
        out_shape=jax.ShapeDtypeStruct((8, 8, 32, depth), bf16),
        in_specs=[anywhere, smem, anywhere, anywhere, vmem, vmem],
        out_specs=anywhere,
        scratch_shapes=[
            pltpu.VMEM((2, 6, 10, 128, depth), bf16),
            pltpu.VMEM((5, 128, 8, depth), bf16),
            pltpu.VMEM((2, 4, 27, 32, 128), bf16),
            pltpu.VMEM((8, 128), f32),
            pltpu.VMEM((4, 8, 128), f32),
            pltpu.VMEM((2, 128, 128), f32),
            pltpu.VMEM((4, 4, 4, 32, depth), bf16),
            dma((5,)),
            dma((2,)),
            dma((2, 3)),
            dma((2, 3)),
            dma((3,)),
            dma((3,)),
            dma((3,)),
            dma((3,)),
            dma((8,)),
            dma((8,)),
            dma((3,)),
            dma((3,)),
            dma,
        ],
        compiler_params=pltpu.CompilerParams(
            collective_id=0, has_side_effects=True, vmem_limit_bytes=60 << 20
        ),
        name="two_convolutions",
    )(
        features,
        column_heights,
        weight_one,
        weight_two,
        bias_one.reshape(1, 32),
        bias_two.reshape(1, 32),
    )
    return gathered.transpose(2, 0, 1, 3)[None]


def solution(mesh):
    placed = (
        P("space", None, None, None, None),
        P(),
        P(None, "chan", None),
        P("chan"),
        P(None, "chan", None),
        P("chan"),
    )
    return jax.shard_map(
        on_device,
        mesh=mesh,
        in_specs=placed,
        out_specs=P("space", "chan", None, None, None),
        check_vma=False,
    )
```

time: 777 us -> 62 us (0.08)
  the two profiles are of different devices: /device:TPU:3 before, /device:TPU:7 now
where the time goes in v1:
time: 62 us; the launch traced here: 61.8 us
  Pallas kernels  59 us (95%)
  local copies, waits for them, and re-layouts  2.78 us (4%)
    pallas_call x1, Pallas kernels, on_device(): pl.pallas_call(functools.partial(kernel, columns // COL_Y, COL_Y), out_sh...  59 us
    broadcast_in_dim x1, local copies, waits for them, and re-layouts, on_device(): return gathered.transpose(2, 0, 1, 3)[None]  2.78 us

profile of v1, /device:TPU:7, one launch (start us, length us, event | category | flops | bytes accessed | tf_op | source)
XLA Modules:
  0.0 61.8 jit_solution(6990605935328269323)
XLA Ops:
  0.0 59.0 %two_convolutions.1 = bf16[8,8,32,256]{3,2,1,0:T(8,128)(2,1)} custom-call(bf16[1,128,8,8,256]{4,3,2,1,0:T(8,128)(2,1)} %feat.1, s32[64]{0:T(128)} %heights.1, bf16[27,32,128]{2,1,0:T(8,128)(2,1)} %w_one.1, bf16[27,32,128]{2,1,0:T(8,128)(2,1)} %w_two.1, f32[1,32]{1,0:T(1,128)} %bitcast.6, f32[1,32]{1,0:T(1,128)} %bitcast.7), custom_call_target="tpu_custom_call" | custom-call | tf_op jit(solution)/shard_map/two_convolutions/pallas_call | solution.py:380
  59.1 2.8 %copy.7 = bf16[1,32,8,8,256]{4,3,2,1,0:T(8,128)(2,1)} copy(bf16[1,32,8,8,256]{4,1,3,2,0:T(8,128)(2,1)} %bitcast.5) | data formatting | bytes 2097152 | tf_op jit(solution)/shard_map/broadcast_in_dim | solution.py:419

commit v2 on v1

v2 whole, which is shorter than its diff:
```python
import functools

import jax
import jax.numpy as jnp
from jax import lax
from jax.experimental import pallas as pl
from jax.experimental.pallas import tpu as pltpu
from jax.sharding import PartitionSpec as P

COL_Y = 8
MESH = pl.DeviceIdType.MESH
DIRECTIONS = [(dx, dy) for dx in (-1, 0, 1) for dy in (-1, 0, 1) if (dx, dy) != (0, 0)]
FIRST_ORDER = [
    (0, 0), (1, 0), (2, 0), (0, 1), (0, 2), (3, 0), (3, 1), (3, 2),
    (3, 3), (2, 3), (1, 3), (0, 3), (1, 1), (2, 1), (1, 2), (2, 2),
]
SECOND_ORDER = [
    (1, 1), (2, 1), (1, 2), (2, 2), (0, 1), (0, 2), (1, 0), (2, 0),
    (0, 0), (1, 3), (2, 3), (0, 3), (3, 1), (3, 2), (3, 0), (3, 3),
]
SECOND_WAITS = [
    (2, [(-1, 0)]),
    (3, [(0, -1)]),
    (4, [(-1, -1), (0, 1)]),
    (5, [(-1, 1)]),
    (6, [(1, 0)]),
    (7, [(1, -1), (1, 1)]),
]


def kernel(
    grid_x,
    grid_y,
    feat,
    heights,
    w_one,
    w_two,
    b_one,
    b_two,
    out,
    xx,
    stage,
    wall,
    bme,
    ball,
    bias,
    obuf,
    feat_sem,
    wl_sem,
    w_send,
    w_recv,
    b_send,
    b_recv,
    f_send,
    f_recv,
    h_send,
    h_recv,
    o_send,
    o_recv,
    o_local,
):
    column = lax.axis_index("space")
    chan = lax.axis_index("chan")
    core = chan % 2
    half = chan // 2
    col_x = column // grid_y
    col_y = column % grid_y
    fine_x = 2 * col_x + core
    fine_y = 2 * col_y + half
    depth = xx.shape[-1]
    base_y = 4 * half
    out_x = 2 * core - 1
    out_y = 2 * half - 1
    has_x = (col_x + out_x >= 0) & (col_x + out_x < grid_x)
    has_y = (col_y + out_y >= 0) & (col_y + out_y < grid_y)

    def device_at(a, b):
        fx, fy = fine_x + a * out_x, fine_y + b * out_y
        return ((fx // 2) * grid_y + fy // 2, (fy % 2) * 2 + fx % 2)

    def if_there(a, b):
        def run(action):
            if a == 1 and b == 1:
                pl.when(has_x & has_y)(action)
            elif a == 1:
                pl.when(has_x)(action)
            elif b == 1:
                pl.when(has_y)(action)
            else:
                action()

        return run

    def remote(src, dst, send_sem, recv_sem, target):
        return pltpu.make_async_remote_copy(
            src_ref=src,
            dst_ref=dst,
            send_sem=send_sem,
            recv_sem=recv_sem,
            device_id=target,
            device_id_type=MESH,
        )

    siblings = [
        (column, (1 - half) * 2 + core),
        (column, half * 2 + 1 - core),
        (column, (1 - half) * 2 + 1 - core),
    ]

    def feature_load(xl):
        return pltpu.make_async_copy(
            feat.at[0, :, 3 * core + xl], stage.at[xl], feat_sem.at[xl]
        )

    def turned(i):
        return 4 * core + (1 - 2 * core) * i

    for i in range(5):
        feature_load(turned(i)).start()
    weights = (w_one, w_two)

    def weight_load(layer):
        return pltpu.make_async_copy(
            weights[layer], wall.at[layer, chan], wl_sem.at[layer]
        )

    for layer in range(2):
        weight_load(layer).start()

    barrier = pltpu.get_barrier_semaphore()
    for a, b in DIRECTIONS:

        @if_there(a, b)
        def _():
            pl.semaphore_signal(
                barrier, inc=1, device_id=device_at(a, b), device_id_type=MESH
            )

    bme[...] = jnp.zeros_like(bme)
    bme[0:1, 0:32] = b_one[...]
    bme[1:2, 0:32] = b_two[...]
    ball[chan] = bme[...]

    live_top = heights[column] * 8
    lanes = lax.broadcasted_iota(jnp.int32, (1, 1, depth), 2)
    live_row = jnp.where(lanes < live_top, 1.0, 0.0).astype(jnp.bfloat16)

    def turn(i):
        xl = turned(i)
        feature_load(xl).wait()
        value = stage[xl] * live_row
        xx[0, xl + 1 - core, 1:9] = jnp.transpose(value, (1, 0, 2))

    def feature_send(a, b, i=None):
        src_x, dst_x = 1 + 3 * core, 5 - 5 * core
        src_y, dst_y = 1 + 7 * half, 9 - 9 * half
        if b == 0:
            run = pl.ds(1 + 3 * half, 5)
            src, dst = xx.at[0, src_x, run], xx.at[0, dst_x, run]
        elif a == 0:
            run = pl.ds(1 - core, 5) if i is None else turned(i) + 1 - core
            src, dst = xx.at[0, run, src_y], xx.at[0, run, dst_y]
        else:
            src, dst = xx.at[0, src_x, src_y], xx.at[0, dst_x, dst_y]
        k = a + 2 * b - 1
        return remote(src, dst, f_send.at[k], f_recv.at[k], device_at(a, b))

    FACES = ((1, 0), (0, 1), (1, 1))

    lax.fori_loop(0, 2, lambda i, carry: (turn(i), carry)[1], 0)

    def there(flag):
        return flag.astype(jnp.int32)

    pl.semaphore_wait(barrier, 3 + 2 * there(has_x) + 2 * there(has_y) + there(has_x & has_y))

    def weight_send(layer, k):
        share = chan if k < 2 else siblings[0][1]
        src = weights[layer] if k < 2 else wall.at[layer, share]
        return remote(
            src,
            wall.at[layer, share],
            w_send.at[layer, k],
            w_recv.at[layer, k],
            siblings[0 if k == 0 else 1],
        )

    def bias_send(k):
        return remote(bme, ball.at[chan], b_send.at[k], b_recv.at[k], siblings[k])

    for k in range(2):
        weight_send(0, k).start()
    for a, b in ((1, 0), (1, 1)):

        @if_there(a, b)
        def _():
            feature_send(a, b).start()

    for i in range(2):

        @if_there(0, 1)
        def _():
            feature_send(0, 1, i).start()

    for k in range(3):
        bias_send(k).start()

    def later_turn(i, carry):
        turn(i)

        @if_there(0, 1)
        def _():
            feature_send(0, 1, i).start()

        return carry

    lax.fori_loop(2, 5, later_turn, 0)

    @pl.when(jnp.logical_not(has_x))
    def _():
        for layer in range(2):

            def clear(y, carry):
                xx[layer, 5 * core, y] = jnp.zeros((xx.shape[3], depth), xx.dtype)
                return carry

            lax.fori_loop(0, 10, clear, 0)

    @pl.when(jnp.logical_not(has_y))
    def _():
        for layer in range(2):

            def clear(x, carry):
                xx[layer, x, 9 * half] = jnp.zeros((xx.shape[3], depth), xx.dtype)
                return carry

            lax.fori_loop(0, 6, clear, 0)

    def relay(layer):
        weight_send(layer, 0).wait_recv()
        weight_send(layer, 2).start()

    relay(0)
    for k in range(2):
        weight_send(1, k).start()

    for k in range(3):
        bias_send(k).wait_recv()
    rows = lax.broadcasted_iota(jnp.int32, (32, 128), 0)
    cols = lax.broadcasted_iota(jnp.int32, (32, 128), 1)
    for layer in range(2):
        for c in range(4):
            spread = jnp.broadcast_to(ball[c, layer : layer + 1, :], (32, 128))
            column_of = jnp.sum(
                jnp.where(rows == cols, spread, 0.0), axis=1, keepdims=True
            )
            bias[layer, 32 * c : 32 * c + 32] = jnp.broadcast_to(column_of, (32, 128))

    def weights_ready(layer):
        weight_load(layer).wait()
        weight_send(layer, 1).wait_recv()
        weight_send(layer, 2).wait_recv()

    weights_ready(0)

    lane = lax.broadcasted_iota(jnp.int32, (128, depth), 1)

    def convolve(layer, px, py):
        rhs = jnp.concatenate(
            [xx[layer, px + i, base_y + py + j] for i in range(3) for j in range(3)],
            axis=0,
        )
        lhs = jnp.concatenate(
            [
                jnp.concatenate([wall[layer, c, 3 * t + k] for t in range(9)], axis=1)
                for k in range(3)
                for c in range(4)
            ],
            axis=0,
        )
        part = jnp.dot(lhs, rhs, preferred_element_type=jnp.float32)
        low = jnp.where(lane == 0, 0.0, pltpu.roll(part[0:128], 1, 1))
        high = jnp.where(lane == depth - 1, 0.0, pltpu.roll(part[256:384], depth - 1, 1))
        column_of = bias[layer]
        total = part[128:256] + low + high + jnp.concatenate([column_of] * (depth // 128), axis=1)
        total = jnp.where(lane < live_top, jnp.maximum(total, 0.0), 0.0)
        return total.astype(jnp.bfloat16)

    def listed(n, table):
        found = table[0]
        for k in range(1, 16):
            if table[k] != table[k - 1]:
                found = found + (table[k] - table[k - 1]) * lax.div(n + (16 - k), 16)
        return found

    def place(order, n):
        u = listed(n, [p[0] for p in order])
        v = listed(n, [p[1] for p in order])
        px = (1 - core) * 3 + out_x * u
        py = (1 - half) * 3 + out_y * v
        return u, v, px, py

    def at_edge(a, b, u, v):
        flag = None
        for side, value in ((a, u), (b, v)):
            if side != 0:
                mine = value == (3 if side == 1 else 0)
                flag = mine if flag is None else flag & mine
        return flag

    def hidden_send(a, b, px, py):
        src_x, src_y = px + 1, py + 1
        dst_x = src_x - 4 * a * out_x
        dst_y = src_y - 4 * b * out_y
        there_y = half if b == 0 else 1 - half
        k = 3 * (a + 1) + b + 1
        return remote(
            xx.at[1, src_x, base_y + src_y],
            xx.at[1, dst_x, 4 * there_y + dst_y],
            h_send.at[k],
            h_recv.at[k],
            device_at(a, b),
        )

    def hidden_whole(a, b, arrived):
        def side(s, outer):
            if s == 0:
                return pl.ds(1, 4)
            edge = 5 * outer if s == 1 else 5 - 5 * outer
            return edge if arrived else 1 + 3 * (outer if s == 1 else 1 - outer)

        x, y = side(a, core), side(b, half)
        y = pl.ds(base_y + 1, 4) if b == 0 else base_y + y
        k = 3 * (a + 1) + b + 1
        return remote(xx.at[1, x, y], xx.at[1, x, y], h_send.at[k], h_recv.at[k], device_at(a, b))

    def output_send(k, px=None, py=None):
        target = siblings[k]
        if px is None:
            src = obuf.at[target[1]]
            dst = out.at[pl.ds(4 * core, 4), pl.ds(4 * half, 4)]
        else:
            src = obuf.at[target[1], px, py]
            dst = out.at[4 * core + px, 4 * half + py]
        return remote(src, dst, o_send.at[k], o_recv.at[k], target)

    def first_pair(t, carry):
        @pl.when(t == 2)
        def _():
            for a, b in FACES:

                @if_there(a, b)
                def _():
                    feature_send(a, b).wait_recv()

        @pl.when(t == 6)
        def _():
            relay(1)

        places = [place(FIRST_ORDER, 2 * t + q) for q in range(2)]
        for u, v, px, py in places:
            xx[1, px + 1, base_y + py + 1] = convolve(0, px, py)
        for u, v, px, py in places:
            for a, b in DIRECTIONS:

                @pl.when(at_edge(a, b, u, v))
                def _():
                    @if_there(a, b)
                    def _():
                        hidden_send(a, b, px, py).start()

        return carry

    lax.fori_loop(0, 8, first_pair, 0)

    weights_ready(1)

    def second_pair(t, carry):
        for step, sides in SECOND_WAITS:

            @pl.when(t == step)
            def _():
                for a, b in sides:

                    @if_there(a, b)
                    def _():
                        hidden_whole(a, b, True).wait_recv()

        places = [place(SECOND_ORDER, 2 * t + q) for q in range(2)]
        for u, v, px, py in places:
            value = convolve(1, px, py)
            for c in range(4):
                obuf[c, px, py] = value[32 * c : 32 * c + 32]
        for u, v, px, py in places:
            for k in (0, 2, 1):
                output_send(k, px, py).start()

        return carry

    lax.fori_loop(0, 8, second_pair, 0)

    own = pltpu.make_async_copy(
        obuf.at[chan], out.at[pl.ds(4 * core, 4), pl.ds(4 * half, 4)], o_local
    )
    own.start()
    for k in range(3):
        bias_send(k).wait_send()
        for layer in range(2):
            weight_send(layer, k).wait_send()
    for a, b in FACES:

        @if_there(a, b)
        def _():
            feature_send(a, b).wait_send()

    for a, b in DIRECTIONS:

        @if_there(a, b)
        def _():
            hidden_whole(a, b, False).wait_send()

    for k in range(3):
        output_send(k).wait_send()

    def arriving(k):
        target = siblings[k]
        there = (pl.ds(4 * (target[1] % 2), 4), pl.ds(4 * (target[1] // 2), 4))
        return remote(obuf.at[chan], out.at[there[0], there[1]], o_send.at[k], o_recv.at[k], target)

    for k in (1, 0, 2):
        arriving(k).wait_recv()
    own.wait()


def on_device(features, column_heights, weight_one, bias_one, weight_two, bias_two):
    columns = lax.axis_size("space")
    depth = features.shape[4]
    bf16, f32 = jnp.bfloat16, jnp.float32
    anywhere = pl.BlockSpec(memory_space=pl.ANY)
    vmem = pl.BlockSpec(memory_space=pltpu.VMEM)
    smem = pl.BlockSpec(memory_space=pltpu.SMEM)
    dma = pltpu.SemaphoreType.DMA
    gathered = pl.pallas_call(
        functools.partial(kernel, columns // COL_Y, COL_Y),
        out_shape=jax.ShapeDtypeStruct((8, 8, 32, depth), bf16),
        in_specs=[anywhere, smem, anywhere, anywhere, vmem, vmem],
        out_specs=anywhere,
        scratch_shapes=[
            pltpu.VMEM((2, 6, 10, 128, depth), bf16),
            pltpu.VMEM((5, 128, 8, depth), bf16),
            pltpu.VMEM((2, 4, 27, 32, 128), bf16),
            pltpu.VMEM((8, 128), f32),
            pltpu.VMEM((4, 8, 128), f32),
            pltpu.VMEM((2, 128, 128), f32),
            pltpu.VMEM((4, 4, 4, 32, depth), bf16),
            dma((5,)),
            dma((2,)),
            dma((2, 3)),
            dma((2, 3)),
            dma((3,)),
            dma((3,)),
            dma((3,)),
            dma((3,)),
            dma((9,)),
            dma((9,)),
            dma((3,)),
            dma((3,)),
            dma,
        ],
        compiler_params=pltpu.CompilerParams(
            collective_id=0, has_side_effects=True, vmem_limit_bytes=60 << 20
        ),
        name="two_convolutions",
    )(
        features,
        column_heights,
        weight_one,
        weight_two,
        bias_one.reshape(1, 32),
        bias_two.reshape(1, 32),
    )
    return gathered.transpose(2, 0, 1, 3)[None]


def solution(mesh):
    placed = (
        P("space", None, None, None, None),
        P(),
        P(None, "chan", None),
        P("chan"),
        P(None, "chan", None),
        P("chan"),
    )
    return jax.shard_map(
        on_device,
        mesh=mesh,
        in_specs=placed,
        out_specs=P("space", "chan", None, None, None),
        check_vma=False,
    )
```

time: 62 us -> 56.8 us (0.916)
  the two profiles are of different devices: /device:TPU:7 before, /device:TPU:206 now
where the time goes in v2:
time: 56.8 us; the launch traced here: 56.7 us
  Pallas kernels  53.9 us (95%)
  local copies, waits for them, and re-layouts  2.78 us (5%)
    pallas_call x1, Pallas kernels, on_device(): pl.pallas_call(functools.partial(kernel, columns // COL_Y, COL_Y), out_sh...  53.9 us
    broadcast_in_dim x1, local copies, waits for them, and re-layouts, on_device(): return gathered.transpose(2, 0, 1, 3)[None]  2.78 us

profile of v2, /device:TPU:206, one launch (start us, length us, event | category | flops | bytes accessed | tf_op | source)
XLA Modules:
  0.0 56.7 jit_solution(10247506267498057327)
XLA Ops:
  0.0 53.9 %two_convolutions.1 = bf16[8,8,32,256]{3,2,1,0:T(8,128)(2,1)} custom-call(bf16[1,128,8,8,256]{4,3,2,1,0:T(8,128)(2,1)} %feat.1, s32[64]{0:T(128)} %heights.1, bf16[27,32,128]{2,1,0:T(8,128)(2,1)} %w_one.1, bf16[27,32,128]{2,1,0:T(8,128)(2,1)} %w_two.1, f32[1,32]{1,0:T(1,128)} %bitcast.6, f32[1,32]{1,0:T(1,128)} %bitcast.7), custom_call_target="tpu_custom_call" | custom-call | tf_op jit(solution)/shard_map/two_convolutions/pallas_call | solution.py:443
  53.9 2.8 %copy.7 = bf16[1,32,8,8,256]{4,3,2,1,0:T(8,128)(2,1)} copy(bf16[1,32,8,8,256]{4,1,3,2,0:T(8,128)(2,1)} %bitcast.5) | data formatting | bytes 2097152 | tf_op jit(solution)/shard_map/broadcast_in_dim | solution.py:482

commit v3 on v2

--- a/solution.py
+++ b/solution.py
@@ -11,21 +11,20 @@
 MESH = pl.DeviceIdType.MESH
 DIRECTIONS = [(dx, dy) for dx in (-1, 0, 1) for dy in (-1, 0, 1) if (dx, dy) != (0, 0)]
 FIRST_ORDER = [
-    (0, 0), (1, 0), (2, 0), (0, 1), (0, 2), (3, 0), (3, 1), (3, 2),
-    (3, 3), (2, 3), (1, 3), (0, 3), (1, 1), (2, 1), (1, 2), (2, 2),
+    [(0, -1), (0, 0), (0, 1), (0, 2)],
+    [(3, 3), (3, 2), (2, 3), (3, 1)],
+    [(1, 3), (3, 0), (0, 3), (3, -1)],
+    [(1, -1), (1, 0), (2, -1), (2, 0)],
+    [(1, 1), (2, 1), (1, 2), (2, 2)],
 ]
 SECOND_ORDER = [
-    (1, 1), (2, 1), (1, 2), (2, 2), (0, 1), (0, 2), (1, 0), (2, 0),
-    (0, 0), (1, 3), (2, 3), (0, 3), (3, 1), (3, 2), (3, 0), (3, 3),
+    [(1, 0), (2, 0), (1, 1), (2, 1)],
+    [(1, 2), (2, 2), (0, 0), (0, 1)],
+    [(0, 2), (1, 3), (2, 3), (0, 3)],
+    [(3, 0), (3, 1), (3, 2), (3, 3)],
 ]
-SECOND_WAITS = [
-    (2, [(-1, 0)]),
-    (3, [(0, -1)]),
-    (4, [(-1, -1), (0, 1)]),
-    (5, [(-1, 1)]),
-    (6, [(1, 0)]),
-    (7, [(1, -1), (1, 1)]),
-]
+SECOND_WAITS = [(1, [(-1, 0)]), (2, [(0, 1), (-1, 1)]), (3, [(1, 0), (1, 1)])]
+HIDDEN = [(-1, 0), (1, 0), (0, 1), (-1, 1), (1, 1)]
 
 
 def kernel(
@@ -155,7 +154,7 @@
         src_x, dst_x = 1 + 3 * core, 5 - 5 * core
         src_y, dst_y = 1 + 7 * half, 9 - 9 * half
         if b == 0:
-            run = pl.ds(1 + 3 * half, 5)
+            run = pl.ds(1 + 2 * half, 6)
             src, dst = xx.at[0, src_x, run], xx.at[0, dst_x, run]
         elif a == 0:
             run = pl.ds(1 - core, 5) if i is None else turned(i) + 1 - core
@@ -286,19 +285,22 @@
         total = jnp.where(lane < live_top, jnp.maximum(total, 0.0), 0.0)
         return total.astype(jnp.bfloat16)
 
-    def listed(n, table):
+    def listed(t, table):
         found = table[0]
-        for k in range(1, 16):
+        for k in range(1, len(table)):
             if table[k] != table[k - 1]:
-                found = found + (table[k] - table[k - 1]) * lax.div(n + (16 - k), 16)
+                found = found + (table[k] - table[k - 1]) * lax.div(t + (8 - k), 8)
         return found
 
-    def place(order, n):
-        u = listed(n, [p[0] for p in order])
-        v = listed(n, [p[1] for p in order])
-        px = (1 - core) * 3 + out_x * u
-        py = (1 - half) * 3 + out_y * v
-        return u, v, px, py
+    def places(order, t):
+        found = []
+        for q in range(4):
+            u = listed(t, [group[q][0] for group in order])
+            v = listed(t, [group[q][1] for group in order])
+            px = (1 - core) * 3 + out_x * u
+            py = (1 - half) * 3 + out_y * v
+            found.append((u, v, px, py))
+        return found
 
     def at_edge(a, b, u, v):
         flag = None
@@ -323,14 +325,13 @@
         )
 
     def hidden_whole(a, b, arrived):
-        def side(s, outer):
-            if s == 0:
-                return pl.ds(1, 4)
-            edge = 5 * outer if s == 1 else 5 - 5 * outer
-            return edge if arrived else 1 + 3 * (outer if s == 1 else 1 - outer)
-
-        x, y = side(a, core), side(b, half)
-        y = pl.ds(base_y + 1, 4) if b == 0 else base_y + y
+        def edge(s, outer):
+            if arrived:
+                return 5 * outer if s == 1 else 5 - 5 * outer
+            return 1 + 3 * (outer if s == 1 else 1 - outer)
+
+        x = pl.ds(1, 4) if a == 0 else edge(a, core)
+        y = pl.ds(base_y + 1 - half, 5) if b == 0 else base_y + edge(b, half)
         k = 3 * (a + 1) + b + 1
         return remote(xx.at[1, x, y], xx.at[1, x, y], h_send.at[k], h_recv.at[k], device_at(a, b))
 
@@ -344,8 +345,8 @@
             dst = out.at[4 * core + px, 4 * half + py]
         return remote(src, dst, o_send.at[k], o_recv.at[k], target)
 
-    def first_pair(t, carry):
-        @pl.when(t == 2)
+    def first_step(t, carry):
+        @pl.when(t == 1)
         def _():
             for a, b in FACES:
 
@@ -353,15 +354,15 @@
                 def _():
                     feature_send(a, b).wait_recv()
 
-        @pl.when(t == 6)
+        @pl.when(t == 3)
         def _():
             relay(1)
 
-        places = [place(FIRST_ORDER, 2 * t + q) for q in range(2)]
-        for u, v, px, py in places:
+        found = places(FIRST_ORDER, t)
+        for u, v, px, py in found:
             xx[1, px + 1, base_y + py + 1] = convolve(0, px, py)
-        for u, v, px, py in places:
-            for a, b in DIRECTIONS:
+        for u, v, px, py in found:
+            for a, b in HIDDEN:
 
                 @pl.when(at_edge(a, b, u, v))
                 def _():
@@ -371,11 +372,11 @@
 
         return carry
 
-    lax.fori_loop(0, 8, first_pair, 0)
+    lax.fori_loop(0, len(FIRST_ORDER), first_step, 0)
 
     weights_ready(1)
 
-    def second_pair(t, carry):
+    def second_step(t, carry):
         for step, sides in SECOND_WAITS:
 
             @pl.when(t == step)
@@ -386,18 +387,18 @@
                     def _():
                         hidden_whole(a, b, True).wait_recv()
 
-        places = [place(SECOND_ORDER, 2 * t + q) for q in range(2)]
-        for u, v, px, py in places:
+        found = places(SECOND_ORDER, t)
+        for u, v, px, py in found:
             value = convolve(1, px, py)
             for c in range(4):
                 obuf[c, px, py] = value[32 * c : 32 * c + 32]
-        for u, v, px, py in places:
+        for u, v, px, py in found:
             for k in (0, 2, 1):
                 output_send(k, px, py).start()
 
         return carry
 
-    lax.fori_loop(0, 8, second_pair, 0)
+    lax.fori_loop(0, len(SECOND_ORDER), second_step, 0)
 
     own = pltpu.make_async_copy(
         obuf.at[chan], out.at[pl.ds(4 * core, 4), pl.ds(4 * half, 4)], o_local
@@ -413,7 +414,7 @@
         def _():
             feature_send(a, b).wait_send()
 
-    for a, b in DIRECTIONS:
+    for a, b in HIDDEN:
 
         @if_there(a, b)
         def _():

time: 56.8 us -> 57.6 us (1.014)
  the two profiles are of different devices: /device:TPU:206 before, /device:TPU:204 now
where the time goes in v3:
time: 57.6 us; the launch traced here: 57.4 us
  Pallas kernels  54.7 us (95%)
  local copies, waits for them, and re-layouts  2.78 us (5%)
    pallas_call x1, Pallas kernels, on_device(): pl.pallas_call(functools.partial(kernel, columns // COL_Y, COL_Y), out_sh...  54.7 us
    broadcast_in_dim x1, local copies, waits for them, and re-layouts, on_device(): return gathered.transpose(2, 0, 1, 3)[None]  2.78 us

profile of v3, /device:TPU:204, one launch (start us, length us, event | category | flops | bytes accessed | tf_op | source)
XLA Modules:
  0.0 57.4 jit_solution(1182966644499296557)
XLA Ops:
  0.0 54.7 %two_convolutions.1 = bf16[8,8,32,256]{3,2,1,0:T(8,128)(2,1)} custom-call(bf16[1,128,8,8,256]{4,3,2,1,0:T(8,128)(2,1)} %feat.1, s32[64]{0:T(128)} %heights.1, bf16[27,32,128]{2,1,0:T(8,128)(2,1)} %w_one.1, bf16[27,32,128]{2,1,0:T(8,128)(2,1)} %w_two.1, f32[1,32]{1,0:T(1,128)} %bitcast.6, f32[1,32]{1,0:T(1,128)} %bitcast.7), custom_call_target="tpu_custom_call" | custom-call | tf_op jit(solution)/shard_map/two_convolutions/pallas_call | solution.py:444
  54.7 2.8 %copy.7 = bf16[1,32,8,8,256]{4,3,2,1,0:T(8,128)(2,1)} copy(bf16[1,32,8,8,256]{4,1,3,2,0:T(8,128)(2,1)} %bitcast.5) | data formatting | bytes 2097152 | tf_op jit(solution)/shard_map/broadcast_in_dim | solution.py:483

commit v4 on v3

--- a/solution.py
+++ b/solution.py
@@ -9,22 +9,21 @@
 
 COL_Y = 8
 MESH = pl.DeviceIdType.MESH
-DIRECTIONS = [(dx, dy) for dx in (-1, 0, 1) for dy in (-1, 0, 1) if (dx, dy) != (0, 0)]
+PARTNERS = [(-1, 0), (0, -1), (-1, -1), (1, 0), (0, 1), (1, 1)]
 FIRST_ORDER = [
     [(0, -1), (0, 0), (0, 1), (0, 2)],
-    [(3, 3), (3, 2), (2, 3), (3, 1)],
-    [(1, 3), (3, 0), (0, 3), (3, -1)],
     [(1, -1), (1, 0), (2, -1), (2, 0)],
+    [(3, 2), (2, 3), (3, 1), (1, 3)],
+    [(3, 3), (3, 0), (0, 3), (3, -1)],
     [(1, 1), (2, 1), (1, 2), (2, 2)],
 ]
 SECOND_ORDER = [
     [(1, 0), (2, 0), (1, 1), (2, 1)],
     [(1, 2), (2, 2), (0, 0), (0, 1)],
-    [(0, 2), (1, 3), (2, 3), (0, 3)],
-    [(3, 0), (3, 1), (3, 2), (3, 3)],
+    [(3, 2), (2, 3), (3, 1), (1, 3)],
+    [(0, 2), (0, 3), (3, 0), (3, 3)],
 ]
-SECOND_WAITS = [(1, [(-1, 0)]), (2, [(0, 1), (-1, 1)]), (3, [(1, 0), (1, 1)])]
-HIDDEN = [(-1, 0), (1, 0), (0, 1), (-1, 1), (1, 1)]
+HIDDEN = [(-1, 0), (1, 0), (0, 1), (1, 1)]
 
 
 def kernel(
@@ -127,7 +126,7 @@
         weight_load(layer).start()
 
     barrier = pltpu.get_barrier_semaphore()
-    for a, b in DIRECTIONS:
+    for a, b in PARTNERS:
 
         @if_there(a, b)
         def _():
@@ -154,10 +153,10 @@
         src_x, dst_x = 1 + 3 * core, 5 - 5 * core
         src_y, dst_y = 1 + 7 * half, 9 - 9 * half
         if b == 0:
-            run = pl.ds(1 + 2 * half, 6)
+            run = pl.ds(1 + base_y, 4)
             src, dst = xx.at[0, src_x, run], xx.at[0, dst_x, run]
         elif a == 0:
-            run = pl.ds(1 - core, 5) if i is None else turned(i) + 1 - core
+            run = pl.ds(1, 4) if i is None else turned(i) + 1 - core
             src, dst = xx.at[0, run, src_y], xx.at[0, run, dst_y]
         else:
             src, dst = xx.at[0, src_x, src_y], xx.at[0, dst_x, dst_y]
@@ -166,12 +165,27 @@
 
     FACES = ((1, 0), (0, 1), (1, 1))
 
+    def passed_on(layer, k, send_sem, recv_sem):
+        if k == 0:
+            rows = pl.ds(3 + 2 * half, 2) if layer == 0 else 4 + half
+            src = dst = xx.at[layer, 5 * core, rows]
+        else:
+            src = xx.at[layer, 4 - 3 * core, 9 * half]
+            dst = xx.at[layer, 5 * core, 9 * half]
+        return remote(src, dst, send_sem, recv_sem, siblings[k])
+
+    def feature_pass(k):
+        return passed_on(0, k, f_send.at[3 + k], f_recv.at[3 + k])
+
+    def hidden_pass(k):
+        return passed_on(1, k, h_send.at[4 + k], h_recv.at[4 + k])
+
     lax.fori_loop(0, 2, lambda i, carry: (turn(i), carry)[1], 0)
 
     def there(flag):
         return flag.astype(jnp.int32)
 
-    pl.semaphore_wait(barrier, 3 + 2 * there(has_x) + 2 * there(has_y) + there(has_x & has_y))
+    pl.semaphore_wait(barrier, 3 + there(has_x) + there(has_y) + there(has_x & has_y))
 
     def weight_send(layer, k):
         share = chan if k < 2 else siblings[0][1]
@@ -213,7 +227,8 @@
 
         return carry
 
-    lax.fori_loop(2, 5, later_turn, 0)
+    lax.fori_loop(2, 4, later_turn, 0)
+    turn(4)
 
     @pl.when(jnp.logical_not(has_x))
     def _():
@@ -308,6 +323,8 @@
             if side != 0:
                 mine = value == (3 if side == 1 else 0)
                 flag = mine if flag is None else flag & mine
+        if (a, b) == (1, 0):
+            flag = flag & (v >= 0)
         return flag
 
     def hidden_send(a, b, px, py):
@@ -315,7 +332,7 @@
         dst_x = src_x - 4 * a * out_x
         dst_y = src_y - 4 * b * out_y
         there_y = half if b == 0 else 1 - half
-        k = 3 * (a + 1) + b + 1
+        k = HIDDEN.index((a, b))
         return remote(
             xx.at[1, src_x, base_y + src_y],
             xx.at[1, dst_x, 4 * there_y + dst_y],
@@ -331,8 +348,11 @@
             return 1 + 3 * (outer if s == 1 else 1 - outer)
 
         x = pl.ds(1, 4) if a == 0 else edge(a, core)
-        y = pl.ds(base_y + 1 - half, 5) if b == 0 else base_y + edge(b, half)
-        k = 3 * (a + 1) + b + 1
+        if b != 0:
+            y = base_y + edge(b, half)
+        else:
+            y = pl.ds(base_y + 1, 4) if a == 1 else pl.ds(base_y + 1 - half, 5)
+        k = HIDDEN.index((a, b))
         return remote(xx.at[1, x, y], xx.at[1, x, y], h_send.at[k], h_recv.at[k], device_at(a, b))
 
     def output_send(k, px=None, py=None):
@@ -346,21 +366,33 @@
         return remote(src, dst, o_send.at[k], o_recv.at[k], target)
 
     def first_step(t, carry):
-        @pl.when(t == 1)
-        def _():
-            for a, b in FACES:
+        @pl.when(t == 2)
+        def _():
+            for k, (a, b) in enumerate(FACES[:2]):
 
                 @if_there(a, b)
                 def _():
                     feature_send(a, b).wait_recv()
+                    feature_pass(k).start()
+
+            relay(1)
 
         @pl.when(t == 3)
         def _():
-            relay(1)
+            for k, (a, b) in enumerate(FACES[:2]):
+
+                @if_there(a, b)
+                def _():
+                    feature_pass(k).wait_recv()
+
+            @if_there(1, 1)
+            def _():
+                feature_send(1, 1).wait_recv()
 
         found = places(FIRST_ORDER, t)
-        for u, v, px, py in found:
-            xx[1, px + 1, base_y + py + 1] = convolve(0, px, py)
+        values = [convolve(0, px, py) for u, v, px, py in found]
+        for (u, v, px, py), value in zip(found, values):
+            xx[1, px + 1, base_y + py + 1] = value
         for u, v, px, py in found:
             for a, b in HIDDEN:
 
@@ -377,19 +409,34 @@
     weights_ready(1)
 
     def second_step(t, carry):
-        for step, sides in SECOND_WAITS:
-
-            @pl.when(t == step)
+        @pl.when(t == 1)
+        def _():
+            hidden_whole(-1, 0, True).wait_recv()
+
+        @pl.when(t == 2)
+        def _():
+            for k, (a, b) in enumerate(FACES[:2]):
+
+                @if_there(a, b)
+                def _():
+                    hidden_whole(a, b, True).wait_recv()
+                    hidden_pass(k).start()
+
+        @pl.when(t == 3)
+        def _():
+            for k, (a, b) in enumerate(FACES[:2]):
+
+                @if_there(a, b)
+                def _():
+                    hidden_pass(k).wait_recv()
+
+            @if_there(1, 1)
             def _():
-                for a, b in sides:
-
-                    @if_there(a, b)
-                    def _():
-                        hidden_whole(a, b, True).wait_recv()
+                hidden_whole(1, 1, True).wait_recv()
 
         found = places(SECOND_ORDER, t)
-        for u, v, px, py in found:
-            value = convolve(1, px, py)
+        values = [convolve(1, px, py) for u, v, px, py in found]
+        for (u, v, px, py), value in zip(found, values):
             for c in range(4):
                 obuf[c, px, py] = value[32 * c : 32 * c + 32]
         for u, v, px, py in found:
@@ -413,6 +460,13 @@
         @if_there(a, b)
         def _():
             feature_send(a, b).wait_send()
+
+    for k, (a, b) in enumerate(FACES[:2]):
+
+        @if_there(a, b)
+        def _():
+            feature_pass(k).wait_send()
+            hidden_pass(k).wait_send()
 
     for a, b in HIDDEN:
 
@@ -460,10 +514,10 @@
             dma((2, 3)),
             dma((3,)),
             dma((3,)),
-            dma((3,)),
-            dma((3,)),
-            dma((9,)),
-            dma((9,)),
+            dma((5,)),
+            dma((5,)),
+            dma((6,)),
+            dma((6,)),
             dma((3,)),
             dma((3,)),
             dma,

time: 57.6 us -> 47.1 us (0.82)
  the two profiles are of different devices: /device:TPU:204 before, /device:TPU:13 now
where the time goes in v4:
time: 47.1 us; the launch traced here: 46.9 us
  Pallas kernels  44.1 us (94%)
  local copies, waits for them, and re-layouts  2.78 us (6%)
    pallas_call x1, Pallas kernels, on_device(): pl.pallas_call(functools.partial(kernel, columns // COL_Y, COL_Y), out_sh...  44.1 us
    broadcast_in_dim x1, local copies, waits for them, and re-layouts, on_device(): return gathered.transpose(2, 0, 1, 3)[None]  2.78 us

profile of v4, /device:TPU:13, one launch (start us, length us, event | category | flops | bytes accessed | tf_op | source)
XLA Modules:
  0.0 46.9 jit_solution(12565015193494629258)
XLA Ops:
  0.0 44.1 %two_convolutions.1 = bf16[8,8,32,256]{3,2,1,0:T(8,128)(2,1)} custom-call(bf16[1,128,8,8,256]{4,3,2,1,0:T(8,128)(2,1)} %feat.1, s32[64]{0:T(128)} %heights.1, bf16[27,32,128]{2,1,0:T(8,128)(2,1)} %w_one.1, bf16[27,32,128]{2,1,0:T(8,128)(2,1)} %w_two.1, f32[1,32]{1,0:T(1,128)} %bitcast.6, f32[1,32]{1,0:T(1,128)} %bitcast.7), custom_call_target="tpu_custom_call" | custom-call | tf_op jit(solution)/shard_map/two_convolutions/pallas_call | solution.py:498
  44.1 2.8 %copy.7 = bf16[1,32,8,8,256]{4,3,2,1,0:T(8,128)(2,1)} copy(bf16[1,32,8,8,256]{4,1,3,2,0:T(8,128)(2,1)} %bitcast.5) | data formatting | bytes 2097152 | tf_op jit(solution)/shard_map/broadcast_in_dim | solution.py:537

commit v5 on v4

--- a/solution.py
+++ b/solution.py
@@ -9,13 +9,13 @@
 
 COL_Y = 8
 MESH = pl.DeviceIdType.MESH
-PARTNERS = [(-1, 0), (0, -1), (-1, -1), (1, 0), (0, 1), (1, 1)]
+PARTNERS = [(-1, 0), (0, -1), (-1, -1), (1, 0), (0, 1)]
 FIRST_ORDER = [
     [(0, -1), (0, 0), (0, 1), (0, 2)],
     [(1, -1), (1, 0), (2, -1), (2, 0)],
+    [(1, 1), (2, 1), (1, 2), (2, 2)],
     [(3, 2), (2, 3), (3, 1), (1, 3)],
     [(3, 3), (3, 0), (0, 3), (3, -1)],
-    [(1, 1), (2, 1), (1, 2), (2, 2)],
 ]
 SECOND_ORDER = [
     [(1, 0), (2, 0), (1, 1), (2, 1)],
@@ -23,7 +23,7 @@
     [(3, 2), (2, 3), (3, 1), (1, 3)],
     [(0, 2), (0, 3), (3, 0), (3, 3)],
 ]
-HIDDEN = [(-1, 0), (1, 0), (0, 1), (1, 1)]
+HIDDEN = [(-1, 0), (1, 0), (0, 1)]
 
 
 def kernel(
@@ -155,37 +155,38 @@
         if b == 0:
             run = pl.ds(1 + base_y, 4)
             src, dst = xx.at[0, src_x, run], xx.at[0, dst_x, run]
-        elif a == 0:
+        else:
             run = pl.ds(1, 4) if i is None else turned(i) + 1 - core
             src, dst = xx.at[0, run, src_y], xx.at[0, run, dst_y]
-        else:
-            src, dst = xx.at[0, src_x, src_y], xx.at[0, dst_x, dst_y]
-        k = a + 2 * b - 1
+        k = b
         return remote(src, dst, f_send.at[k], f_recv.at[k], device_at(a, b))
 
-    FACES = ((1, 0), (0, 1), (1, 1))
+    FACES = ((1, 0), (0, 1))
 
     def passed_on(layer, k, send_sem, recv_sem):
         if k == 0:
             rows = pl.ds(3 + 2 * half, 2) if layer == 0 else 4 + half
             src = dst = xx.at[layer, 5 * core, rows]
-        else:
+        elif k == 1:
             src = xx.at[layer, 4 - 3 * core, 9 * half]
             dst = xx.at[layer, 5 * core, 9 * half]
-        return remote(src, dst, send_sem, recv_sem, siblings[k])
+        else:
+            src = xx.at[layer, 5 * core, 1 + 7 * half]
+            dst = xx.at[layer, 5 * core, 9 - 9 * half]
+        return remote(src, dst, send_sem, recv_sem, device_at(0, 1) if k == 2 else siblings[k])
 
     def feature_pass(k):
-        return passed_on(0, k, f_send.at[3 + k], f_recv.at[3 + k])
+        return passed_on(0, k, f_send.at[2 + k], f_recv.at[2 + k])
 
     def hidden_pass(k):
-        return passed_on(1, k, h_send.at[4 + k], h_recv.at[4 + k])
+        return passed_on(1, k, h_send.at[3 + k], h_recv.at[3 + k])
 
     lax.fori_loop(0, 2, lambda i, carry: (turn(i), carry)[1], 0)
 
     def there(flag):
         return flag.astype(jnp.int32)
 
-    pl.semaphore_wait(barrier, 3 + there(has_x) + there(has_y) + there(has_x & has_y))
+    pl.semaphore_wait(barrier, 3 + there(has_x) + there(has_y))
 
     def weight_send(layer, k):
         share = chan if k < 2 else siblings[0][1]
@@ -203,11 +204,10 @@
 
     for k in range(2):
         weight_send(0, k).start()
-    for a, b in ((1, 0), (1, 1)):
-
-        @if_there(a, b)
-        def _():
-            feature_send(a, b).start()
+
+    @if_there(1, 0)
+    def _():
+        feature_send(1, 0).start()
 
     for i in range(2):
 
@@ -323,8 +323,6 @@
             if side != 0:
                 mine = value == (3 if side == 1 else 0)
                 flag = mine if flag is None else flag & mine
-        if (a, b) == (1, 0):
-            flag = flag & (v >= 0)
         return flag
 
     def hidden_send(a, b, px, py):
@@ -351,7 +349,7 @@
         if b != 0:
             y = base_y + edge(b, half)
         else:
-            y = pl.ds(base_y + 1, 4) if a == 1 else pl.ds(base_y + 1 - half, 5)
+            y = pl.ds(base_y + 1 - half, 5)
         k = HIDDEN.index((a, b))
         return remote(xx.at[1, x, y], xx.at[1, x, y], h_send.at[k], h_recv.at[k], device_at(a, b))
 
@@ -366,20 +364,26 @@
         return remote(src, dst, o_send.at[k], o_recv.at[k], target)
 
     def first_step(t, carry):
-        @pl.when(t == 2)
-        def _():
-            for k, (a, b) in enumerate(FACES[:2]):
+        @pl.when(t == 3)
+        def _():
+            for k, (a, b) in enumerate(FACES):
 
                 @if_there(a, b)
                 def _():
                     feature_send(a, b).wait_recv()
                     feature_pass(k).start()
 
+                if k == 0:
+
+                    @if_there(1, 1)
+                    def _():
+                        feature_pass(2).start()
+
             relay(1)
 
-        @pl.when(t == 3)
-        def _():
-            for k, (a, b) in enumerate(FACES[:2]):
+        @pl.when(t == 4)
+        def _():
+            for k, (a, b) in enumerate(FACES):
 
                 @if_there(a, b)
                 def _():
@@ -387,7 +391,7 @@
 
             @if_there(1, 1)
             def _():
-                feature_send(1, 1).wait_recv()
+                feature_pass(2).wait_recv()
 
         found = places(FIRST_ORDER, t)
         values = [convolve(0, px, py) for u, v, px, py in found]
@@ -415,24 +419,29 @@
 
         @pl.when(t == 2)
         def _():
-            for k, (a, b) in enumerate(FACES[:2]):
+            for k, (a, b) in enumerate(FACES):
 
                 @if_there(a, b)
                 def _():
                     hidden_whole(a, b, True).wait_recv()
-                    hidden_pass(k).start()
+                    if k == 1:
+                        hidden_pass(1).start()
+
+                if k == 0:
+
+                    @if_there(1, 1)
+                    def _():
+                        hidden_pass(2).start()
 
         @pl.when(t == 3)
         def _():
-            for k, (a, b) in enumerate(FACES[:2]):
-
-                @if_there(a, b)
-                def _():
-                    hidden_pass(k).wait_recv()
+            @if_there(0, 1)
+            def _():
+                hidden_pass(1).wait_recv()
 
             @if_there(1, 1)
             def _():
-                hidden_whole(1, 1, True).wait_recv()
+                hidden_pass(2).wait_recv()
 
         found = places(SECOND_ORDER, t)
         values = [convolve(1, px, py) for u, v, px, py in found]
@@ -461,12 +470,18 @@
         def _():
             feature_send(a, b).wait_send()
 
-    for k, (a, b) in enumerate(FACES[:2]):
+    for k, (a, b) in enumerate(FACES):
 
         @if_there(a, b)
         def _():
             feature_pass(k).wait_send()
-            hidden_pass(k).wait_send()
+            if k == 1:
+                hidden_pass(1).wait_send()
+
+    @if_there(1, 1)
+    def _():
+        feature_pass(2).wait_send()
+        hidden_pass(2).wait_send()
 
     for a, b in HIDDEN:
 
@@ -485,6 +500,12 @@
     for k in (1, 0, 2):
         arriving(k).wait_recv()
     own.wait()
+
+
+def settle(gathered, out):
+    rows = out.shape[2]
+    for x in range(rows):
+        out[0, :, x] = jnp.transpose(gathered[pl.program_id(0) * rows + x], (1, 0, 2))
 
 
 def on_device(features, column_heights, weight_one, bias_one, weight_two, bias_two):
@@ -534,7 +555,14 @@
         bias_one.reshape(1, 32),
         bias_two.reshape(1, 32),
     )
-    return gathered.transpose(2, 0, 1, 3)[None]
+    return pl.pallas_call(
+        settle,
+        grid=(2,),
+        out_shape=jax.ShapeDtypeStruct((1, 32, 8, 8, depth), bf16),
+        in_specs=[vmem],
+        out_specs=pl.BlockSpec((1, 32, 4, 8, depth), lambda x: (0, 0, x, 0, 0)),
+        name="settle",
+    )(gathered)
 
 
 def solution(mesh):

time: 47.1 us -> 45 us (0.955)
  the two profiles are of different devices: /device:TPU:13 before, /device:TPU:51 now
where the time goes in v5:
time: 45 us; the launch traced here: 44.9 us
  Pallas kernels  44.9 us (100%)
    pallas_call x1, Pallas kernels, on_device(): pl.pallas_call(functools.partial(kernel, columns // COL_Y, COL_Y), out_sh...  42.5 us
    pallas_call x1, Pallas kernels, on_device(): pl.pallas_call(settle, grid=(2,), out_shape=jax.ShapeDtypeStruct((1, 32,...  2.35 us

profile of v5, /device:TPU:51, one launch (start us, length us, event | category | flops | bytes accessed | tf_op | source)
XLA Modules:
  0.0 44.9 jit_solution(4522502426049346354)
XLA Ops:
  0.0 42.5 %two_convolutions.1.gathered = bf16[8,8,32,256]{3,2,1,0:T(8,128)(2,1)} custom-call(bf16[1,128,8,8,256]{4,3,2,1,0:T(8,128)(2,1)} %feat.1, s32[64]{0:T(128)} %heights.1, bf16[27,32,128]{2,1,0:T(8,128)(2,1)} %w_one.1, bf16[27,32,128]{2,1,0:T(8,128)(2,1)} %w_two.1, f32[1,32]{1,0:T(1,128)} %bitcast.2, f32[1,32]{1,0:T(1,128)} %bitcast.3), custom_call_target="tpu_custom_call" | custom-call | tf_op jit(solution)/shard_map/two_convolutions/pallas_call | solution.py:519
  42.5 2.3 %settle.1 = bf16[1,32,8,8,256]{4,3,2,1,0:T(8,128)(2,1)} custom-call(bf16[8,8,32,256]{3,2,1,0:T(8,128)(2,1)} %two_convolutions.1.gathered), custom_call_target="tpu_custom_call" | custom-call | tf_op jit(solution)/shard_map/settle/pallas_call | solution.py:558

commit v6 on v5

--- a/solution.py
+++ b/solution.py
@@ -14,8 +14,8 @@
     [(0, -1), (0, 0), (0, 1), (0, 2)],
     [(1, -1), (1, 0), (2, -1), (2, 0)],
     [(1, 1), (2, 1), (1, 2), (2, 2)],
-    [(3, 2), (2, 3), (3, 1), (1, 3)],
-    [(3, 3), (3, 0), (0, 3), (3, -1)],
+    [(3, 1), (3, 2), (2, 3), (1, 3)],
+    [(3, -1), (3, 0), (3, 3), (0, 3)],
 ]
 SECOND_ORDER = [
     [(1, 0), (2, 0), (1, 1), (2, 1)],
@@ -181,7 +181,7 @@
     def hidden_pass(k):
         return passed_on(1, k, h_send.at[3 + k], h_recv.at[3 + k])
 
-    lax.fori_loop(0, 2, lambda i, carry: (turn(i), carry)[1], 0)
+    lax.fori_loop(0, 1, lambda i, carry: (turn(i), carry)[1], 0)
 
     def there(flag):
         return flag.astype(jnp.int32)
@@ -209,7 +209,7 @@
     def _():
         feature_send(1, 0).start()
 
-    for i in range(2):
+    for i in range(1):
 
         @if_there(0, 1)
         def _():
@@ -227,7 +227,7 @@
 
         return carry
 
-    lax.fori_loop(2, 4, later_turn, 0)
+    lax.fori_loop(1, 4, later_turn, 0)
     turn(4)
 
     @pl.when(jnp.logical_not(has_x))
@@ -449,12 +449,13 @@
             for c in range(4):
                 obuf[c, px, py] = value[32 * c : 32 * c + 32]
         for u, v, px, py in found:
-            for k in (0, 2, 1):
+            for k in (0, 2):
                 output_send(k, px, py).start()
 
         return carry
 
     lax.fori_loop(0, len(SECOND_ORDER), second_step, 0)
+    output_send(1).start()
 
     own = pltpu.make_async_copy(
         obuf.at[chan], out.at[pl.ds(4 * core, 4), pl.ds(4 * half, 4)], o_local
@@ -502,10 +503,17 @@
     own.wait()
 
 
-def settle(gathered, out):
-    rows = out.shape[2]
-    for x in range(rows):
-        out[0, :, x] = jnp.transpose(gathered[pl.program_id(0) * rows + x], (1, 0, 2))
+def settle(gathered, out, held, turned, load_sems, store_sems):
+    loads = [pltpu.make_async_copy(gathered.at[x], held.at[x], load_sems.at[x]) for x in range(8)]
+    stores = [pltpu.make_async_copy(turned.at[x], out.at[0, :, x], store_sems.at[x]) for x in range(8)]
+    for load in loads:
+        load.start()
+    for x in range(8):
+        loads[x].wait()
+        turned[x] = jnp.transpose(held[x], (1, 0, 2))
+        stores[x].start()
+    for store in stores:
+        store.wait()
 
 
 def on_device(features, column_heights, weight_one, bias_one, weight_two, bias_two):
@@ -557,10 +565,15 @@
     )
     return pl.pallas_call(
         settle,
-        grid=(2,),
         out_shape=jax.ShapeDtypeStruct((1, 32, 8, 8, depth), bf16),
-        in_specs=[vmem],
-        out_specs=pl.BlockSpec((1, 32, 4, 8, depth), lambda x: (0, 0, x, 0, 0)),
+        in_specs=[anywhere],
+        out_specs=anywhere,
+        scratch_shapes=[
+            pltpu.VMEM((8, 8, 32, depth), bf16),
+            pltpu.VMEM((8, 32, 8, depth), bf16),
+            dma((8,)),
+            dma((8,)),
+        ],
         name="settle",
     )(gathered)
 

time: 45 us -> 44.1 us (0.980)
  Pallas kernels: 44.9 us -> 43.9 us
    pallas_call x1, Pallas kernels: 42.5 us -> 41.8 us  [on_device(): pl.pallas_call(functools.partial(kernel, columns // COL_Y, COL_Y), out_sh...]
where the time goes in v6:
time: 44.1 us; the launch traced here: 43.9 us
  Pallas kernels  43.9 us (100%)
    pallas_call x1, Pallas kernels, on_device(): pl.pallas_call(functools.partial(kernel, columns // COL_Y, COL_Y), out_sh...  41.8 us
    pallas_call x1, Pallas kernels, on_device(): pl.pallas_call(settle, out_shape=jax.ShapeDtypeStruct((1, 32, 8, 8, depth...  2.12 us

profile of v6, /device:TPU:51, one launch (start us, length us, event | category | flops | bytes accessed | tf_op | source)
XLA Modules:
  0.0 43.9 jit_solution(10693528498610210965)
XLA Ops:
  0.0 41.8 %two_convolutions.1.gathered = bf16[8,8,32,256]{3,2,1,0:T(8,128)(2,1)} custom-call(bf16[1,128,8,8,256]{4,3,2,1,0:T(8,128)(2,1)} %feat.1, s32[64]{0:T(128)} %heights.1, bf16[27,32,128]{2,1,0:T(8,128)(2,1)} %w_one.1, bf16[27,32,128]{2,1,0:T(8,128)(2,1)} %w_two.1, f32[1,32]{1,0:T(1,128)} %bitcast.2, f32[1,32]{1,0:T(1,128)} %bitcast.3), custom_call_target="tpu_custom_call" | custom-call | tf_op jit(solution)/shard_map/two_convolutions/pallas_call | solution.py:527
  41.8 2.1 %settle.1 = bf16[1,32,8,8,256]{4,3,2,1,0:T(8,128)(2,1)} custom-call(bf16[8,8,32,256]{3,2,1,0:T(8,128)(2,1)} %two_convolutions.1.gathered), custom_call_target="tpu_custom_call" | custom-call | tf_op jit(solution)/shard_map/settle/pallas_call | solution.py:566

commit v7 on v6

--- a/solution.py
+++ b/solution.py
@@ -105,6 +105,15 @@
         (column, (1 - half) * 2 + 1 - core),
     ]
 
+    barrier = pltpu.get_barrier_semaphore()
+    for a, b in PARTNERS:
+
+        @if_there(a, b)
+        def _():
+            pl.semaphore_signal(
+                barrier, inc=1, device_id=device_at(a, b), device_id_type=MESH
+            )
+
     def feature_load(xl):
         return pltpu.make_async_copy(
             feat.at[0, :, 3 * core + xl], stage.at[xl], feat_sem.at[xl]
@@ -124,15 +133,6 @@
 
     for layer in range(2):
         weight_load(layer).start()
-
-    barrier = pltpu.get_barrier_semaphore()
-    for a, b in PARTNERS:
-
-        @if_there(a, b)
-        def _():
-            pl.semaphore_signal(
-                barrier, inc=1, device_id=device_at(a, b), device_id_type=MESH
-            )
 
     bme[...] = jnp.zeros_like(bme)
     bme[0:1, 0:32] = b_one[...]

time: 44.1 us -> 44.7 us (1.014)
  Pallas kernels: 43.9 us -> 44.6 us
    pallas_call x1, Pallas kernels: 41.8 us -> 42.5 us  [on_device(): pl.pallas_call(functools.partial(kernel, columns // COL_Y, COL_Y), out_sh...]
where the time goes in v7:
time: 44.7 us; the launch traced here: 44.6 us
  Pallas kernels  44.6 us (100%)
    pallas_call x1, Pallas kernels, on_device(): pl.pallas_call(functools.partial(kernel, columns // COL_Y, COL_Y), out_sh...  42.5 us
    pallas_call x1, Pallas kernels, on_device(): pl.pallas_call(settle, out_shape=jax.ShapeDtypeStruct((1, 32, 8, 8, depth...  2.12 us

profile of v7, /device:TPU:51, one launch (start us, length us, event | category | flops | bytes accessed | tf_op | source)
XLA Modules:
  0.0 44.6 jit_solution(1680295015847031651)
XLA Ops:
  0.0 42.5 %two_convolutions.1.gathered = bf16[8,8,32,256]{3,2,1,0:T(8,128)(2,1)} custom-call(bf16[1,128,8,8,256]{4,3,2,1,0:T(8,128)(2,1)} %feat.1, s32[64]{0:T(128)} %heights.1, bf16[27,32,128]{2,1,0:T(8,128)(2,1)} %w_one.1, bf16[27,32,128]{2,1,0:T(8,128)(2,1)} %w_two.1, f32[1,32]{1,0:T(1,128)} %bitcast.2, f32[1,32]{1,0:T(1,128)} %bitcast.3), custom_call_target="tpu_custom_call" | custom-call | tf_op jit(solution)/shard_map/two_convolutions/pallas_call | solution.py:527
  42.5 2.1 %settle.1 = bf16[1,32,8,8,256]{4,3,2,1,0:T(8,128)(2,1)} custom-call(bf16[8,8,32,256]{3,2,1,0:T(8,128)(2,1)} %two_convolutions.1.gathered), custom_call_target="tpu_custom_call" | custom-call | tf_op jit(solution)/shard_map/settle/pallas_call | solution.py:566
